TPU v7x, 32 devices: a whole 2x2x4 slice. The times are simulated.
32 devices in a mesh: fsdp: 4 (over y, x), ctx: 4 (over z), tp: 2 (over core).
Axes of the slice: x: 2, y: 2, z: 4, core: 2. Of those that a mesh axis runs over, the one named last changes fastest.
Arguments:
- inputs: bfloat16 [4, 1024, 2048], P('fsdp', 'ctx'), may hold values from -6 to 6
- positions: int32 [4, 1024], P('fsdp', 'ctx'), may hold values from 0 to 1535, as said below
- blocks: int32 [4, 1024], P('fsdp', 'ctx'), may hold values from 0 to 7, never falling along the last dimension, each value on 1 to 256 neighbouring positions
- cotangent: bfloat16 [4, 1024, 2048], P('fsdp', 'ctx'), may hold values from -6 to 6
- attn_gain: bfloat16 [2048], P('fsdp'), may hold values from 0.099609375 to 1.8984375
- w_query: bfloat16 [2048, 2048], P('fsdp', 'tp'), may hold values from -0.125 to 0.125
- w_key: bfloat16 [2048, 256], P('fsdp', 'tp'), may hold values from -0.125 to 0.125
- w_value: bfloat16 [2048, 256], P('fsdp', 'tp'), may hold values from -0.125 to 0.125
- w_out: bfloat16 [2048, 2048], P('tp', 'fsdp'), may hold values from -1 to 1
- mlp_gain: bfloat16 [2048], P('fsdp'), may hold values from 0.099609375 to 1.8984375
- w_gate: bfloat16 [2048, 5632], P('fsdp', 'tp'), may hold values from -0.125 to 0.125
- w_up: bfloat16 [2048, 5632], P('fsdp', 'tp'), may hold values from -0.125 to 0.125
- w_down: bfloat16 [5632, 2048], P('tp', 'fsdp'), may hold values from -0.078125 to 0.078125
Outputs:
- output: bfloat16 [4, 1024, 2048], P('fsdp', 'ctx')
- input_grad: float32 [4, 1024, 2048], P('fsdp', 'ctx')
- attn_gain_grad: float32 [2048], P('fsdp')
- query_grad: float32 [2048, 2048], P('fsdp', 'tp')
- key_grad: float32 [2048, 256], P('fsdp', 'tp')
- value_grad: float32 [2048, 256], P('fsdp', 'tp')
- out_grad: float32 [2048, 2048], P('tp', 'fsdp')
- mlp_gain_grad: float32 [2048], P('fsdp')
- gate_grad: float32 [2048, 5632], P('fsdp', 'tp')
- up_grad: float32 [2048, 5632], P('fsdp', 'tp')
- down_grad: float32 [5632, 2048], P('tp', 'fsdp')
Inputs may be any that keep to these rules, and one draw needn't show every extreme that they name: `positions`: positions start at 0 and rise by 1 or 2 from each token to the next along a sequence; in every sequence exactly 512 of these steps are 2. `blocks`: block ids never fall along a sequence; every block holds 1 to 256 tokens.
All inputs are finite; a program needn't handle non-finite values.
Results may differ from a plain program's by a relative error of at most 0.023.
Values may be sent and summed in bfloat16 or wider, within the bound.
A program may use at most 320 MiB of HBM per device.

v0:
```python
import math

import jax
import jax.numpy as jnp
from jax import lax
from jax.sharding import PartitionSpec as P

HD = 64


EPSILON = 1e-05
NEGATIVE = -1e30


def angles(positions, head_size):
    half_size = head_size // 2
    frequency = jnp.exp(
        jnp.arange(half_size, dtype=jnp.float32) * (-2.0 * math.log(10000.0) / head_size)
    )
    turned = positions.astype(jnp.float32)[:, None] * frequency[None, :]
    return (jnp.cos(turned)[:, None, :], jnp.sin(turned)[:, None, :])


def rotate(values, cosine, sine_turn):
    half_size = values.shape[-1] // 2
    first_half = values[..., :half_size]
    second_half = values[..., half_size:]
    return jnp.concatenate(
        [
            first_half * cosine - second_half * sine_turn,
            second_half * cosine + first_half * sine_turn,
        ],
        axis=-1,
    )


def masked_scores(query_four, key_block, key_ids, query_ids, factor):
    scores = (
        jnp.einsum("tkgd,skd->kgts", query_four, key_block, preferred_element_type=jnp.float32)
        * factor
    )
    allowed = key_ids[None, :] <= query_ids[:, None]
    return (jnp.where(allowed, scores, NEGATIVE), allowed)


def norm_back(upstream, normed, scale, gain):
    weighted = upstream * gain
    return scale * (weighted - normed * jnp.mean(weighted * normed, axis=-1, keepdims=True))


def local(
    inputs,
    positions,
    blocks,
    cotangent,
    attn_gain,
    w_query,
    w_key,
    w_value,
    w_out,
    mlp_gain,
    w_gate,
    w_up,
    w_down,
):
    token_rows = inputs[0].astype(jnp.float32)
    place_row = positions[0]
    own_ids = blocks[0]
    back_low = cotangent[0]
    back_full = back_low.astype(jnp.float32)
    tokens = token_rows.shape[0]
    gain_one, query_w, key_w, value_w, gain_two, gate_w, up_w = (
        lax.all_gather(attn_gain, "fsdp", axis=0, tiled=True),
        lax.all_gather(w_query, "fsdp", axis=0, tiled=True),
        lax.all_gather(w_key, "fsdp", axis=0, tiled=True),
        lax.all_gather(w_value, "fsdp", axis=0, tiled=True),
        lax.all_gather(mlp_gain, "fsdp", axis=0, tiled=True),
        lax.all_gather(w_gate, "fsdp", axis=0, tiled=True),
        lax.all_gather(w_up, "fsdp", axis=0, tiled=True),
    )
    out_w, down_w = (
        lax.all_gather(w_out, "fsdp", axis=1, tiled=True),
        lax.all_gather(w_down, "fsdp", axis=1, tiled=True),
    )
    gain_one = gain_one.astype(jnp.float32)
    gain_two = gain_two.astype(jnp.float32)
    scale_one = lax.rsqrt(jnp.mean(token_rows * token_rows, axis=-1, keepdims=True) + EPSILON)
    normed_one = token_rows * scale_one
    input_one = (normed_one * gain_one).astype(jnp.bfloat16)
    query_pre = jnp.dot(input_one, query_w, preferred_element_type=jnp.float32)
    key_pre = jnp.dot(input_one, key_w, preferred_element_type=jnp.float32)
    value_low = jnp.dot(input_one, value_w, preferred_element_type=jnp.float32).astype(jnp.bfloat16)
    cosine, sine_turn = angles(place_row, HD)
    query_rot = rotate(query_pre.reshape(tokens, -1, HD), cosine, sine_turn).astype(jnp.bfloat16)
    key_rot = rotate(key_pre.reshape(tokens, -1, HD), cosine, sine_turn).astype(jnp.bfloat16)
    kv_heads = key_rot.shape[1]
    grouping = query_rot.shape[1] // kv_heads
    query_four = query_rot.reshape(tokens, kv_heads, grouping, HD)
    all_keys, all_values, all_ids = (
        lax.all_gather(key_rot.reshape(tokens, kv_heads * HD), "ctx", axis=0, tiled=True),
        lax.all_gather(value_low, "ctx", axis=0, tiled=True),
        lax.all_gather(own_ids, "ctx", axis=0, tiled=True),
    )
    length = all_keys.shape[0]
    block_rows = math.gcd(length, 512)
    block_total = length // block_rows
    key_blocks = all_keys.reshape(block_total, block_rows, kv_heads, HD)
    value_blocks = all_values.reshape(block_total, block_rows, kv_heads, HD)
    id_blocks = all_ids.reshape(block_total, block_rows)
    factor = 1.0 / math.sqrt(HD)

    def stats_step(carry_pair, block_item):
        running_top, running_sum = carry_pair
        key_block, key_ids = block_item
        scores, allowed = masked_scores(query_four, key_block, key_ids, own_ids, factor)
        new_top = jnp.maximum(running_top, jnp.max(scores, axis=-1))
        fresh = jnp.where(allowed, jnp.exp(scores - new_top[..., None]), 0.0)
        new_sum = running_sum * jnp.exp(running_top - new_top) + jnp.sum(fresh, axis=-1)
        return ((new_top, new_sum), None)

    start_top = jnp.full((kv_heads, grouping, tokens), NEGATIVE, jnp.float32)
    (row_top, row_sum), _ = lax.scan(
        stats_step, (start_top, jnp.zeros_like(start_top)), (key_blocks, id_blocks)
    )

    def probabilities(key_block, key_ids):
        scores, allowed = masked_scores(query_four, key_block, key_ids, own_ids, factor)
        return jnp.where(allowed, jnp.exp(scores - row_top[..., None]) / row_sum[..., None], 0.0)

    def value_step(mixed_sum, block_item):
        key_block, value_block, key_ids = block_item
        weights_low = probabilities(key_block, key_ids).astype(jnp.bfloat16)
        return (
            mixed_sum
            + jnp.einsum(
                "kgts,skd->tkgd", weights_low, value_block, preferred_element_type=jnp.float32
            ),
            None,
        )

    attended, _ = lax.scan(
        value_step,
        jnp.zeros((tokens, kv_heads, grouping, HD), jnp.float32),
        (key_blocks, value_blocks, id_blocks),
    )
    attended_low = attended.astype(jnp.bfloat16).reshape(tokens, -1)
    hidden = token_rows + lax.psum(
        jnp.dot(attended_low, out_w, preferred_element_type=jnp.float32).astype(jnp.bfloat16), "tp"
    ).astype(jnp.float32)
    scale_two = lax.rsqrt(jnp.mean(hidden * hidden, axis=-1, keepdims=True) + EPSILON)
    normed_two = hidden * scale_two
    input_two = (normed_two * gain_two).astype(jnp.bfloat16)
    gate = jnp.dot(input_two, gate_w, preferred_element_type=jnp.float32)
    up_proj = jnp.dot(input_two, up_w, preferred_element_type=jnp.float32)
    sigmoid_gate = jax.nn.sigmoid(gate)
    silu_gate = gate * sigmoid_gate
    activation = (silu_gate * up_proj).astype(jnp.bfloat16)
    mlp_sum = lax.psum(
        jnp.dot(activation, down_w, preferred_element_type=jnp.float32).astype(jnp.bfloat16), "tp"
    ).astype(jnp.float32)
    output = (hidden + mlp_sum).astype(jnp.bfloat16)
    act_grad = jnp.einsum("td,fd->tf", back_low, down_w, preferred_element_type=jnp.float32)
    down_grad_t = jnp.einsum("td,tf->df", back_low, activation, preferred_element_type=jnp.float32)
    gate_back = (act_grad * up_proj * sigmoid_gate * (1.0 + gate * (1.0 - sigmoid_gate))).astype(
        jnp.bfloat16
    )
    up_back = (act_grad * silu_gate).astype(jnp.bfloat16)
    gate_grad = jnp.einsum("td,tf->df", input_two, gate_back, preferred_element_type=jnp.float32)
    up_grad = jnp.einsum("td,tf->df", input_two, up_back, preferred_element_type=jnp.float32)
    two_partial = jnp.einsum(
        "tf,df->td", gate_back, gate_w, preferred_element_type=jnp.float32
    ) + jnp.einsum("tf,df->td", up_back, up_w, preferred_element_type=jnp.float32)
    input_two_grad = lax.psum(two_partial.astype(jnp.bfloat16), "tp").astype(jnp.float32)
    gain_two_grad = jnp.sum(input_two_grad * normed_two, axis=0)
    hidden_grad = back_full + norm_back(input_two_grad, normed_two, scale_two, gain_two)
    hidden_low = hidden_grad.astype(jnp.bfloat16)
    out_grad_t = jnp.einsum(
        "td,tc->dc", hidden_low, attended_low, preferred_element_type=jnp.float32
    )
    attended_grad = (
        jnp.einsum("td,cd->tc", hidden_low, out_w, preferred_element_type=jnp.float32)
        .astype(jnp.bfloat16)
        .reshape(tokens, kv_heads, grouping, HD)
    )
    row_delta = jnp.einsum("tkgd,tkgd->kgt", attended_grad.astype(jnp.float32), attended)

    def back_step(query_sum, block_item):
        key_block, value_block, key_ids = block_item
        weights_full = probabilities(key_block, key_ids)
        weight_grad = jnp.einsum(
            "tkgd,skd->kgts", attended_grad, value_block, preferred_element_type=jnp.float32
        )
        score_grad = (weights_full * (weight_grad - row_delta[..., None])).astype(jnp.bfloat16)
        value_part = jnp.einsum(
            "kgts,tkgd->skd",
            weights_full.astype(jnp.bfloat16),
            attended_grad,
            preferred_element_type=jnp.float32,
        )
        key_part = (
            jnp.einsum("kgts,tkgd->skd", score_grad, query_four, preferred_element_type=jnp.float32)
            * factor
        )
        query_sum = (
            query_sum
            + jnp.einsum(
                "kgts,skd->tkgd", score_grad, key_block, preferred_element_type=jnp.float32
            )
            * factor
        )
        return (query_sum, (key_part, value_part))

    query_grad_rot, (key_parts, value_parts) = lax.scan(
        back_step,
        jnp.zeros((tokens, kv_heads, grouping, HD), jnp.float32),
        (key_blocks, value_blocks, id_blocks),
    )
    key_total, value_total = (
        lax.psum_scatter(
            key_parts.reshape(length, kv_heads * HD).astype(jnp.bfloat16),
            "ctx",
            scatter_dimension=0,
            tiled=True,
        ).astype(jnp.float32),
        lax.psum_scatter(
            value_parts.reshape(length, kv_heads * HD).astype(jnp.bfloat16),
            "ctx",
            scatter_dimension=0,
            tiled=True,
        ).astype(jnp.float32),
    )
    query_back = (
        rotate(query_grad_rot.reshape(tokens, kv_heads * grouping, HD), cosine, -sine_turn)
        .reshape(tokens, -1)
        .astype(jnp.bfloat16)
    )
    key_back = (
        rotate(key_total.reshape(tokens, kv_heads, HD), cosine, -sine_turn)
        .reshape(tokens, -1)
        .astype(jnp.bfloat16)
    )
    value_back = value_total.astype(jnp.bfloat16)
    query_grad = jnp.einsum("td,tc->dc", input_one, query_back, preferred_element_type=jnp.float32)
    key_grad = jnp.einsum("td,tc->dc", input_one, key_back, preferred_element_type=jnp.float32)
    value_grad = jnp.einsum("td,tc->dc", input_one, value_back, preferred_element_type=jnp.float32)
    one_partial = jnp.einsum("tc,dc->td", query_back, query_w, preferred_element_type=jnp.float32)
    one_partial = one_partial + jnp.einsum(
        "tc,dc->td", key_back, key_w, preferred_element_type=jnp.float32
    )
    one_partial = one_partial + jnp.einsum(
        "tc,dc->td", value_back, value_w, preferred_element_type=jnp.float32
    )
    input_one_grad = lax.psum(one_partial.astype(jnp.bfloat16), "tp").astype(jnp.float32)
    gain_one_grad = jnp.sum(input_one_grad * normed_one, axis=0)
    input_grad = hidden_grad + norm_back(input_one_grad, normed_one, scale_one, gain_one)
    shares = (
        lax.psum_scatter(
            gain_one_grad.astype(jnp.bfloat16), "fsdp", scatter_dimension=0, tiled=True
        ).astype(jnp.float32),
        lax.psum_scatter(
            query_grad.astype(jnp.bfloat16), "fsdp", scatter_dimension=0, tiled=True
        ).astype(jnp.float32),
        lax.psum_scatter(
            key_grad.astype(jnp.bfloat16), "fsdp", scatter_dimension=0, tiled=True
        ).astype(jnp.float32),
        lax.psum_scatter(
            value_grad.astype(jnp.bfloat16), "fsdp", scatter_dimension=0, tiled=True
        ).astype(jnp.float32),
        lax.psum_scatter(
            out_grad_t.astype(jnp.bfloat16), "fsdp", scatter_dimension=0, tiled=True
        ).astype(jnp.float32),
        lax.psum_scatter(
            gain_two_grad.astype(jnp.bfloat16), "fsdp", scatter_dimension=0, tiled=True
        ).astype(jnp.float32),
        lax.psum_scatter(
            gate_grad.astype(jnp.bfloat16), "fsdp", scatter_dimension=0, tiled=True
        ).astype(jnp.float32),
        lax.psum_scatter(
            up_grad.astype(jnp.bfloat16), "fsdp", scatter_dimension=0, tiled=True
        ).astype(jnp.float32),
        lax.psum_scatter(
            down_grad_t.astype(jnp.bfloat16), "fsdp", scatter_dimension=0, tiled=True
        ).astype(jnp.float32),
    )
    shares = (
        lax.psum(shares[0].astype(jnp.bfloat16), "ctx").astype(jnp.float32),
        lax.psum(shares[1].astype(jnp.bfloat16), "ctx").astype(jnp.float32),
        lax.psum(shares[2].astype(jnp.bfloat16), "ctx").astype(jnp.float32),
        lax.psum(shares[3].astype(jnp.bfloat16), "ctx").astype(jnp.float32),
        lax.psum(shares[4].astype(jnp.bfloat16), "ctx").astype(jnp.float32),
        lax.psum(shares[5].astype(jnp.bfloat16), "ctx").astype(jnp.float32),
        lax.psum(shares[6].astype(jnp.bfloat16), "ctx").astype(jnp.float32),
        lax.psum(shares[7].astype(jnp.bfloat16), "ctx").astype(jnp.float32),
        lax.psum(shares[8].astype(jnp.bfloat16), "ctx").astype(jnp.float32),
    )
    return (
        output[None],
        input_grad[None],
        shares[0],
        shares[1],
        shares[2],
        shares[3],
        shares[4].T,
        shares[5],
        shares[6],
        shares[7],
        shares[8].T,
    )


def solution(mesh):
    return jax.shard_map(
        local,
        mesh=mesh,
        in_specs=(
            P("fsdp", "ctx", None),
            P("fsdp", "ctx"),
            P("fsdp", "ctx"),
            P("fsdp", "ctx", None),
            P("fsdp"),
            P("fsdp", "tp"),
            P("fsdp", "tp"),
            P("fsdp", "tp"),
            P("tp", "fsdp"),
            P("fsdp"),
            P("fsdp", "tp"),
            P("fsdp", "tp"),
            P("tp", "fsdp"),
        ),
        out_specs=(
            P("fsdp", "ctx", None),
            P("fsdp", "ctx", None),
            P("fsdp"),
            P("fsdp", "tp"),
            P("fsdp", "tp"),
            P("fsdp", "tp"),
            P("tp", "fsdp"),
            P("fsdp"),
            P("fsdp", "tp"),
            P("fsdp", "tp"),
            P("tp", "fsdp"),
        ),
        check_vma=False,
    )
```

profile of v0, /device:TPU:0, one launch (start us, length us, event | category | flops | bytes accessed | tf_op | source)
XLA Modules:
  0.0 1577.6 jit_solution(1991943502405839874)
XLA Ops:
  8.8 11.5 all_gather.37
  20.3 8.1 all-gather.1
  29.2 14.4 all_gather.38
  44.3 10.7 all-gather
  56.2 13.0 all_gather.40
  70.9 13.8 all_gather.41
  84.9 6.4 copy.57
  95.1 19.0 %while.39 = (s32[]{:T(128)}, f32[2,8,256]{2,1,0:T(8,128)S(1)}, f32[2,8,256]{2,1,0:T(8,128)S(1)}, s32[2,512]{1,0:T(2,128)S(1)}, s32[1,256]{1,0:T(1,128)S(1)}, /*i...) while((s32[]{:T(128)}, f32[2,8,256]{2,1,0:T(8,128)S(1)}, ...), condition=%wide.region_4.5_spmd.clone, body=%wide.region_1.4_spmd.clone.sunk | while | flops 285364224 | bytes 18046072 | solution.py:122
  95.3 4.6 fusion.177
  99.9 4.8 select_reduce_fusion.2
  105.0 4.6 fusion.177
  109.6 4.5 select_reduce_fusion.2
  114.1 9.6 while.40
  118.4 5.2 fusion.183
  125.1 4.6 convolution_convert_fusion.5
  131.6 8.4 all-gather.2
  139.9 8.3 all-reduce.11.cloned.1.call-done
  151.5 113.6 %all-gather.13.cloned.1.call-done = bf16[2048,2816]{1,0:T(8,128)(2,1)} async-done(((bf16[512,2816]{1,0:T(8,128)(2,1)}), bf16[2048,2816]{1,0:T(8,128)(2,1)}) %all-gather.13.cloned.1.call-update) | async-done | bytes 11534352 | tf_op jit(solution)/shard_map/all_gather | solution.py:78
  265.1 9.4 fusion.109
  274.4 106.3 %all-gather.15.cloned.1.call-done = bf16[2048,2816]{1,0:T(8,128)(2,1)} async-done(((bf16[512,2816]{1,0:T(8,128)(2,1)}), bf16[2048,2816]{1,0:T(8,128)(2,1)}) %all-gather.15.cloned.1.call-update) | async-done | bytes 11534352 | tf_op jit(solution)/shard_map/all_gather | solution.py:79
  380.8 9.0 fusion.110
  389.7 106.5 %all-gather.17.cloned.1.call-done = bf16[2816,2048]{1,0:T(8,128)(2,1)} async-done(((bf16[2816,512]{1,0:T(8,128)(2,1)}), bf16[2816,2048]{1,0:T(8,128)(2,1)}) %all-gather.17.cloned.1.call-update) | async-done | bytes 11534352 | tf_op jit(solution)/shard_map/all_gather | solution.py:83
  496.3 11.5 multiply_convert_fusion
  507.7 7.1 fusion.111
  514.8 8.4 fusion.68
  523.4 19.7 %all-reduce.13.cloned.1.call-done = bf16[256,2048]{1,0:T(8,128)(2,1)} async-done(((bf16[256,2048]{1,0:T(8,128)(2,1)}), bf16[256,2048]{1,0:T(8,128)(2,1)}) %all-reduce.13.cloned.1.call-update) | async-done | bytes 1048592 | tf_op jit(solution)/shard_map/psum | solution.py:173
  546.3 4.6 convolution_convert_fusion.8
  553.5 35.6 %while.41 = (s32[]{:T(128)}, f32[256,2,8,64]{0,3,2,1:T(8,128)S(1)}, bf16[2,512,2,64]{1,3,2,0:T(8,128)(2,1)}, bf16[2,512,2,64]{1,3,2,0:T(8,128)(2,1)}, bf16[2,512...) while((s32[]{:T(128)}, f32[256,2,8,64]{0,3,2,1:T(8,128)S(1)}, ...), condition=%wide.region_13.14_spmd.clone, body=%wide.region_12.13_spmd.clone.sunk | while | flops 1362034688 | bytes 98753912 | solution.py:213
  565.8 4.9 fusion.198
  583.5 4.9 fusion.198
  593.2 18.9 %reduce-scatter.10.cloned.1.call-done = bf16[256,128]{0,1:T(8,128)(2,1)} async-done(((bf16[1024,128]{0,1:T(8,128)(2,1)}), bf16[256,128]{0,1:T(8,128)(2,1)}) %reduce-scatter.10.cloned.1.call-update) | async-done | bytes 65552 | tf_op jit(solution)/shard_map/reduce_scatter | solution.py:219
  614.5 18.4 %reduce-scatter.12.cloned.1.call-done = bf16[256,128]{0,1:T(8,128)(2,1)} async-done(((bf16[1024,128]{0,1:T(8,128)(2,1)}), bf16[256,128]{0,1:T(8,128)(2,1)}) %reduce-scatter.12.cloned.1.call-update) | async-done | bytes 65552 | tf_op jit(solution)/shard_map/reduce_scatter | solution.py:225
  635.3 6.0 convolution_convert_fusion.2
  646.2 7.5 convolution_convert_fusion.1
  653.8 7.3 convolution_convert_fusion
  662.4 7.4 convert_bitcast_fusion
  671.1 8.7 convolution_convert_fusion.4
  686.6 56.1 %reduce-scatter.20.cloned.1.call-done = bf16[512,1024]{1,0:T(8,128)(2,1)} async-done(((bf16[2048,1024]{1,0:T(8,128)(2,1)}), bf16[512,1024]{1,0:T(8,128)(2,1)}) %reduce-scatter.20.cloned.1.call-update) | async-done | bytes 1048592 | tf_op jit(solution)/shard_map/reduce_scatter | solution.py:269
  742.7 56.5 %reduce-scatter.14.cloned.1.call-done = bf16[512,1024]{1,0:T(8,128)(2,1)} async-done(((bf16[2048,1024]{1,0:T(8,128)(2,1)}), bf16[512,1024]{1,0:T(8,128)(2,1)}) %reduce-scatter.14.cloned.1.call-update) | async-done | bytes 1048592 | tf_op jit(solution)/shard_map/reduce_scatter | solution.py:260
  799.2 115.1 %reduce-scatter.22.cloned.1.call-done = bf16[512,2816]{1,0:T(8,128)(2,1)} async-done(((bf16[2048,2816]{1,0:T(8,128)(2,1)}), bf16[512,2816]{1,0:T(8,128)(2,1)}) %reduce-scatter.22.cloned.1.call-update) | async-done | bytes 2883600 | tf_op jit(solution)/shard_map/reduce_scatter | solution.py:275
  914.3 115.1 %reduce-scatter.24.cloned.1.call-done = bf16[512,2816]{1,0:T(8,128)(2,1)} async-done(((bf16[2048,2816]{1,0:T(8,128)(2,1)}), bf16[512,2816]{1,0:T(8,128)(2,1)}) %reduce-scatter.24.cloned.1.call-update) | async-done | bytes 2883600 | tf_op jit(solution)/shard_map/reduce_scatter | solution.py:278
  1029.4 115.1 %reduce-scatter.26.cloned.1.call-done = bf16[512,2816]{0,1:T(8,128)(2,1)} async-done(((bf16[2048,2816]{0,1:T(8,128)(2,1)}), bf16[512,2816]{0,1:T(8,128)(2,1)}) %reduce-scatter.26.cloned.1.call-update) | async-done | bytes 2883600 | tf_op jit(solution)/shard_map/reduce_scatter | solution.py:281
  1146.4 22.2 %all-reduce.17.cloned.1.call-done = (bf16[256,2048]{1,0:T(8,128)(2,1)}, bf16[256,2048]{1,0:T(8,128)(2,1)}) async-done(((bf16[256,2048]{1,0:T(8,128)(2,1)}, bf16[256,2048]{1,0:T(8,128)(2,1)}), (bf16[256,2048]{1,0:T(8,128)(2,1)}, bf16[256,2048]{1,0:T(8,128)(2,1)})) %all-reduce.17.cloned.1.call-update) | async-done | bytes 2097168 | tf_op jit(solution)/shard_map/psum | solution.py:158
  1170.7 10.3 all-reduce.4
  1181.1 12.3 all-reduce.2
  1194.6 5.5 fusion.75
  1200.1 353.1 %all-reduce.15.cloned.1.call-done = (bf16[1024,512]{0,1:T(8,128)(2,1)}, bf16[512,1024]{1,0:T(8,128)(2,1)}, bf16[512,128]{1,0:T(8,128)(2,1)}, bf16[512,128]{1,0:T...) async-done(((bf16[1024,512]{0,1:T(8,128)(2,1)}, bf16[512,1024]{1,0:T(8,128)(2,1)}, bf16[512,128]{1,0:T(8,128)(2,1)}, ...) | async-done | bytes 11010064 | tf_op jit(solution)/shard_map/psum | solution.py:290
  1559.1 4.9 convert_element_type.271
  (243 shorter events, 92.1 us)
Async XLA Ops:
  7.2 13.1 copy-start.44
  7.2 21.2 %copy-start.2 = (bf16[1,256,2048]{2,1,0:T(8,128)(2,1)S(1)}, bf16[1,256,2048]{2,1,0:T(8,128)(2,1)}, u32[]{:S(2)}) copy-start(bf16[1,256,2048]{2,1,0:T(8,128)(2,1)} %param.19) | copy-start | bytes 3145732
  7.2 77.7 %all-gather.9.cloned.1.call-start = ((), (), s32[]{:S(2)}) async-start(), calls=%async_computation.9 | async-start | bytes 5242880 | tf_op jit(solution)/shard_map/all_gather | solution.py:74
  7.9 117.1 %all-gather.11.cloned.1.call-start = ((), (), s32[]{:S(2)}) async-start(), calls=%async_computation.10 | async-start | bytes 5242880 | tf_op jit(solution)/shard_map/all_gather | solution.py:82
  8.7 139.6 %all-reduce.11.cloned.1.call-start = ((), (), s32[]{:S(2)}) async-start(), calls=%async_computation.11 | async-start | bytes 2097152 | tf_op jit(solution)/shard_map/psum | solution.py:147
  20.3 23.6 %copy-start.19 = (bf16[2048,128]{1,0:T(8,128)(2,1)}, bf16[2048,128]{1,0:T(8,128)(2,1)S(1)}, u32[]{:S(2)}) copy-start(bf16[2048,128]{1,0:T(8,128)(2,1)S(1)} %all_gather.37) | copy-start | bytes 1572868
  28.4 63.0 %copy-start.29 = (f32[4,1,512]{2,1,0:T(1,128)}, f32[4,1,512]{2,1,0:T(1,128)S(1)}, u32[]{:S(2)}) copy-start(f32[4,1,512]{2,1,0:T(1,128)S(1)} %convert_element_type.277) | copy-start | bytes 24580
  28.7 62.7 %copy-start.41 = (f32[256]{0:T(256)}, f32[256]{0:T(256)S(1)}, u32[]{:S(2)}) copy-start(f32[256]{0:T(256)S(1)} %add_rsqrt_fusion.1) | copy-start | bytes 3076
  28.7 15.6 copy-start.31
  28.7 27.4 %copy-start.37 = (bf16[512,128]{1,0:T(8,128)(2,1)S(1)}, bf16[512,128]{1,0:T(8,128)(2,1)}, u32[]{:S(2)}) copy-start(bf16[512,128]{1,0:T(8,128)(2,1)} %param.25) | copy-start | bytes 393220
  55.0 15.0 copy-start.46
  69.2 15.5 copy-start.8
  70.8 24.1 %copy-start.24 = (f32[256,32]{0,1:T(8,128)}, f32[256,32]{0,1:T(8,128)S(1)}, u32[]{:S(2)}) copy-start(f32[256,32]{0,1:T(8,128)S(1)} %get-tuple-element.472) | copy-start | bytes 98308
  123.7 6.0 copy-start.14
  125.0 4.6 copy-start.26
  129.7 135.4 %all-gather.13.cloned.1.call-start = ((), (), s32[]{:S(2)}) async-start(), calls=%async_computation.12 | async-start | bytes 14417920 | tf_op jit(solution)/shard_map/all_gather | solution.py:78
  130.3 250.5 %all-gather.15.cloned.1.call-start = ((), (), s32[]{:S(2)}) async-start(), calls=%async_computation.13 | async-start | bytes 14417920 | tf_op jit(solution)/shard_map/all_gather | solution.py:79
  130.9 365.4 %all-gather.17.cloned.1.call-start = ((), (), s32[]{:S(2)}) async-start(), calls=%async_computation.14 | async-start | bytes 14417920 | tf_op jit(solution)/shard_map/all_gather | solution.py:83
  131.5 411.6 %all-reduce.13.cloned.1.call-start = ((), (), s32[]{:S(2)}) async-start(), calls=%async_computation.15 | async-start | bytes 2097152 | tf_op jit(solution)/shard_map/psum | solution.py:173
  151.5 229.2 %copy-start.6 = (bf16[256,2048]{1,0:T(8,128)(2,1)S(1)}, bf16[256,2048]{1,0:T(8,128)(2,1)}, u32[]{:S(2)}) copy-start(bf16[256,2048]{1,0:T(8,128)(2,1)} %multiply_convert_fusion.3) | copy-start | bytes 3145732
  507.7 7.1 copy-start.22
  507.7 7.1 copy-start.21
  523.3 88.8 %reduce-scatter.10.cloned.1.call-start = ((), (), s32[]{:S(2)}) async-start(), calls=%async_computation.16 | async-start | bytes 327680 | tf_op jit(solution)/shard_map/reduce_scatter | solution.py:219
  556.4 4.5 copy-start.1
  565.8 4.9 copy-start.33
  574.1 4.5 copy-start.1
  583.5 4.9 copy-start.33
  589.1 23.9 %copy-start.25 = (f32[256,32]{0,1:T(8,128)S(1)}, f32[256,32]{0,1:T(8,128)}, u32[]{:S(2)}) copy-start(f32[256,32]{0,1:T(8,128)} %copy-done.24) | copy-start | bytes 98308
  589.1 23.9 %copy-start.28 = (f32[256,32]{0,1:T(8,128)S(1)}, f32[256,32]{0,1:T(8,128)}, u32[]{:S(2)}) copy-start(f32[256,32]{0,1:T(8,128)} %get-tuple-element.470) | copy-start | bytes 98308
  589.1 23.9 %copy-start.30 = (f32[4,1,512]{2,1,0:T(1,128)S(1)}, f32[4,1,512]{2,1,0:T(1,128)}, u32[]{:S(2)}) copy-start(f32[4,1,512]{2,1,0:T(1,128)} %copy-done.29) | copy-start | bytes 24580
  589.1 24.0 %copy-start.42 = (f32[256]{0:T(256)S(1)}, f32[256]{0:T(256)}, u32[]{:S(2)}) copy-start(f32[256]{0:T(256)} %copy-done.41) | copy-start | bytes 3076
  591.1 41.9 %reduce-scatter.12.cloned.1.call-start = ((), (), s32[]{:S(2)}) async-start(), calls=%async_computation.17 | async-start | bytes 327680 | tf_op jit(solution)/shard_map/reduce_scatter | solution.py:225
  593.1 90.7 %reduce-scatter.16.cloned.1.call-start = ((), (), s32[]{:S(2)}) async-start(), calls=%async_computation.19 | async-start | bytes 655360 | tf_op jit(solution)/shard_map/reduce_scatter | solution.py:263
  614.5 20.8 %copy-start.27 = (bf16[256,2,8,64]{0,3,2,1:T(8,128)(2,1)S(1)}, bf16[256,2,8,64]{0,3,2,1:T(8,128)(2,1)}, u32[]{:S(2)}) copy-start(bf16[256,2,8,64]{0,3,2,1:T(8,128)(2,1)} %copy-done.26) | copy-start | bytes 1572868
  614.5 72.1 %reduce-scatter.18.cloned.1.call-start = ((), (), s32[]{:S(2)}) async-start(), calls=%async_computation.20 | async-start | bytes 655360 | tf_op jit(solution)/shard_map/reduce_scatter | solution.py:266
  635.2 107.5 %reduce-scatter.20.cloned.1.call-start = ((), (), s32[]{:S(2)}) async-start(), calls=%async_computation.21 | async-start | bytes 5242880 | tf_op jit(solution)/shard_map/reduce_scatter | solution.py:269
  641.3 157.9 %reduce-scatter.14.cloned.1.call-start = ((), (), s32[]{:S(2)}) async-start(), calls=%async_computation.18 | async-start | bytes 5242880 | tf_op jit(solution)/shard_map/reduce_scatter | solution.py:260
  645.0 269.3 %reduce-scatter.22.cloned.1.call-start = ((), (), s32[]{:S(2)}) async-start(), calls=%async_computation.22 | async-start | bytes 14417920 | tf_op jit(solution)/shard_map/reduce_scatter | solution.py:275
  653.8 375.6 %reduce-scatter.24.cloned.1.call-start = ((), (), s32[]{:S(2)}) async-start(), calls=%async_computation.23 | async-start | bytes 14417920 | tf_op jit(solution)/shard_map/reduce_scatter | solution.py:278
  661.2 483.4 %reduce-scatter.26.cloned.1.call-start = ((), (), s32[]{:S(2)}) async-start(), calls=%async_computation.24 | async-start | bytes 14417920 | tf_op jit(solution)/shard_map/reduce_scatter | solution.py:281
  669.8 498.8 %all-reduce.17.cloned.1.call-start = ((), (), s32[]{:S(2)}) async-start(), calls=%async_computation.26 | async-start | bytes 4194304 | tf_op jit(solution)/shard_map/psum | solution.py:158
  671.1 8.7 copy-start.13
  683.7 869.4 %all-reduce.15.cloned.1.call-start = ((), (), s32[]{:S(2)}) async-start(), calls=%async_computation.25 | async-start | bytes 22020096 | tf_op jit(solution)/shard_map/psum | solution.py:290
  1144.5 26.1 %copy-start.43 = (bf16[2048]{0:T(1024)(128)(2,1)S(1)}, bf16[2048]{0:T(1024)(128)(2,1)}, u32[]{:S(2)}) copy-start(bf16[2048]{0:T(1024)(128)(2,1)} %get-tuple-element.380) | copy-start | bytes 12292
  1144.6 50.0 %copy-start.5 = (bf16[256,2048]{1,0:T(8,128)(2,1)S(1)}, bf16[256,2048]{1,0:T(8,128)(2,1)}, u32[]{:S(2)}) copy-start(bf16[256,2048]{1,0:T(8,128)(2,1)} %all-reduce.11.cloned.1.call-done) | copy-start | bytes 3145732
  1553.1 3.6 copy-start.38
  1553.1 4.3 copy-start.23
  1559.1 4.9 copy-start.17
  (25 other events, 50.7 us)
Sparse Core Ops, SparseCore 0:
  9.9 59.6 all-gather.8
  71.4 52.5 all-gather.10
  129.8 18.3 all-reduce.10
  150.1 114.9 all-gather.12
  266.9 113.7 all-gather.14
  382.6 113.6 all-gather.16
  523.4 19.5 all-reduce.12
  591.2 20.8 reduce-scatter.9
  615.0 17.8 reduce-scatter.11
  635.6 23.0 reduce-scatter.15
  661.8 24.7 reduce-scatter.17
  690.0 52.6 reduce-scatter.19
  746.5 52.6 reduce-scatter.13
  802.2 112.1 reduce-scatter.21
  917.3 112.0 reduce-scatter.23
  1032.4 112.0 reduce-scatter.25
  1147.3 21.2 all-reduce.16
  1172.3 380.7 all-reduce.14
where the time goes:
time: 1590 us; the launch traced here: 1580 us
  waiting for transfers between devices  1230 us (77%)
  matrix products  157 us (10%)
  blocking collectives  102 us (6%)
  other arithmetic  46.7 us (3%)
  local copies, waits for them, and re-layouts  23.8 us (1%)
  between operations  16 us (1%)
    psum x1, waiting for transfers between devices, local(): lax.psum(shares[4].astype(jnp.bfloat16), 'ctx').astype(jnp.float32)  353 us
    reduce_scatter x1, waiting for transfers between devices, local(): lax.psum_scatter(gate_grad.astype(jnp.bfloat16), 'fsdp', scatter_dimensio...  115 us
    reduce_scatter x1, waiting for transfers between devices, local(): lax.psum_scatter(down_grad_t.astype(jnp.bfloat16), 'fsdp', scatter_dimens...  115 us
    reduce_scatter x1, waiting for transfers between devices, local(): lax.psum_scatter(up_grad.astype(jnp.bfloat16), 'fsdp', scatter_dimension=...  115 us
    all_gather x1, waiting for transfers between devices, local(): lax.all_gather(w_gate, 'fsdp', axis=0, tiled=True)  114 us
    all_gather x1, waiting for transfers between devices, local(): lax.all_gather(w_down, 'fsdp', axis=1, tiled=True)  107 us
    all_gather x1, waiting for transfers between devices, local(): lax.all_gather(w_up, 'fsdp', axis=0, tiled=True)  106 us
    reduce_scatter x1, waiting for transfers between devices, local(): lax.psum_scatter(query_grad.astype(jnp.bfloat16), 'fsdp', scatter_dimensi...  56.5 us
  transfers between devices with their start and end apart: 18, of which 15 were waited for; matrix products, arithmetic and copies ran while one was open for 8% of the time, Pallas kernels for 0%

commit v1 on v0

v1 whole, which is shorter than its diff:
```python
import functools
import math

import jax
import jax.numpy as jnp
from jax import lax
from jax.experimental import pallas as pl
from jax.experimental.pallas import tpu as pltpu
from jax.sharding import PartitionSpec as P

HD = 64
EPSILON = 1e-05
NEGATIVE = -1e30
BF = jnp.bfloat16
F32 = jnp.float32


def dot(a, b, ca, cb):
    return lax.dot_general(a, b, (((ca,), (cb,)), ((), ())), preferred_element_type=F32)


def angles(positions):
    half = HD // 2
    frequency = jnp.exp(jnp.arange(half, dtype=F32) * (-2.0 * math.log(10000.0) / HD))
    turned = positions.astype(F32)[:, None] * frequency[None, :]
    return jnp.cos(turned)[:, None, :], jnp.sin(turned)[:, None, :]


def rotate(values, cosine, sine):
    half = HD // 2
    a, b = values[..., :half], values[..., half:]
    return jnp.concatenate([a * cosine - b * sine, b * cosine + a * sine], axis=-1)


def gated(values, after):
    return lax.optimization_barrier((values, after))[0]


def local(n, m, inputs, positions, blocks, cotangent, attn_gain, w_query, w_key, w_value, w_out, mlp_gain, w_gate, w_up, w_down):
    f = lax.axis_index("fsdp")
    z = lax.axis_index("ctx")
    t = lax.axis_index("tp")
    tokens, width = inputs.shape[1:]
    half = width // 2
    peers = range(1, n)

    def plane(x, k):
        return x if k == 0 else lax.ppermute(x, "fsdp", [(i, i ^ k) for i in range(n)])

    def column(x, k):
        return x if k == 0 else lax.ppermute(x, "ctx", [(i, i ^ k) for i in range(m)])

    def swap(x):
        return lax.ppermute(x, "tp", [(0, 1), (1, 0)])

    def part(x, index, axis):
        size = x.shape[axis] // n
        return lax.dynamic_slice_in_dim(x, index * size, size, axis)

    def mine(x, which):
        return lax.dynamic_slice_in_dim(x, which * half, half, x.ndim - 1)

    def place(pieces, axis):
        size = pieces[0].shape[axis]
        shape = list(pieces[0].shape)
        shape[axis] = size * n
        whole = jnp.zeros(shape, pieces[0].dtype)
        for k in range(n):
            whole = lax.dynamic_update_slice_in_dim(whole, pieces[k], (f ^ k) * size, axis)
        return whole

    def join(own, other):
        return jnp.where(t == 0, jnp.concatenate([own, other], -1), jnp.concatenate([other, own], -1))

    def gather(x):
        rows = jnp.concatenate([plane(x, k) for k in range(n)], 0)
        return join(rows, swap(rows))

    def scatter(partial):
        own = mine(partial, t) + swap(mine(partial.astype(BF), 1 - t)).astype(F32)
        low = own.astype(BF)
        total = own[:tokens]
        for k in peers:
            total = total + plane(low[k * tokens : (k + 1) * tokens], k).astype(F32)
        return total

    def row_mean(own):
        own = jnp.sum(own, -1)
        return ((own + swap(own)) / width)[:, None]

    x = inputs[0].astype(F32)
    gains = jnp.stack([attn_gain, mlp_gain])
    gains = place([plane(gains, k) for k in range(n)], 1).astype(F32)
    marks = jnp.stack([positions[0], blocks[0]])
    marks = [plane(marks, k) for k in range(n)]
    place_rows = jnp.concatenate([mk[0] for mk in marks])
    query_ids = jnp.stack([mk[1] for mk in marks])
    scale_one = lax.rsqrt(jnp.mean(x * x, axis=-1, keepdims=True) + EPSILON)
    x_half = mine(x, t)
    hat_one = x_half * scale_one
    gain_one, gain_two = mine(gains[0:1], t), mine(gains[1:2], t)
    xn_one = gather((hat_one * gain_one).astype(BF))

    heads = w_query.shape[1] // HD // n
    cols = heads * HD
    kv_pair = jnp.concatenate([w_key, w_value], 1)
    kv_heads = w_key.shape[1] // HD
    w_qkv = place([plane(jnp.concatenate([part(w_query, f ^ k, 1), kv_pair], 1), k) for k in range(n)], 0)
    wo = gated(w_out, xn_one)
    wo = place([plane(part(wo, f ^ k, 0), k) for k in range(n)], 1)
    gate_up = gated((w_gate, w_up), xn_one)
    gate_up = [plane(jnp.stack([part(gate_up[0], f ^ k, 1), part(gate_up[1], f ^ k, 1)]), k) for k in range(n)]
    wg = place([g[0] for g in gate_up], 0)
    wu = place([g[1] for g in gate_up], 0)

    qkv = dot(xn_one, w_qkv, 1, 0)
    cosine, sine = angles(place_rows)
    kv_here = (heads * f) // ((w_query.shape[1] // HD) // kv_heads)

    def pick(both):
        out = both[:, :HD]
        for g in range(1, kv_heads):
            out = jnp.where(kv_here == g, both[:, g * HD : (g + 1) * HD], out)
        return out

    kw = kv_heads * HD
    query = rotate(qkv[:, :cols].reshape(-1, heads, HD), cosine, sine).astype(BF)
    key = rotate(pick(qkv[:, cols : cols + kw])[:, None, :], cosine, sine)[:, 0, :].astype(BF)
    value = pick(qkv[:, cols + kw :]).astype(BF)
    key_value = jnp.concatenate([key, value], 1).reshape(n, tokens, 2 * HD)
    kv_all = jnp.concatenate([column(key_value, k) for k in range(m)], 1)
    ids_all = jnp.concatenate([column(query_ids, k) for k in range(m)], 1)
    keys, values = kv_all[..., :HD], kv_all[..., HD:]
    factor = 1.0 / math.sqrt(HD)
    query = query.reshape(n, tokens, heads, HD)
    allowed = (ids_all[:, None, :] <= query_ids[:, :, None])[:, None]
    scores = jnp.einsum("nthd,nsd->nhts", query, keys, preferred_element_type=F32) * factor
    scores = jnp.where(allowed, scores, NEGATIVE)
    top = jnp.max(scores, -1, keepdims=True)
    raw = jnp.where(allowed, jnp.exp(scores - top), 0.0)
    weights = raw / jnp.sum(raw, -1, keepdims=True)
    weights_low = weights.astype(BF)
    attended = jnp.einsum("nhts,nsd->nthd", weights_low, values, preferred_element_type=F32)
    attended_low = attended.astype(BF).reshape(n * tokens, cols)

    hidden = x_half + scatter(dot(attended_low, wo, 1, 0))
    scale_two = lax.rsqrt(row_mean(hidden * hidden) + EPSILON)
    hat_two = hidden * scale_two
    xn_two = gather((hat_two * gain_two).astype(BF))
    cot = gather(gated(mine(cotangent[0], t), wg))
    wd = gated(w_down, wg)
    wd = place([plane(part(wd, f ^ k, 0), k) for k in range(n)], 1)
    gate = dot(xn_two, wg, 1, 0)
    up = dot(xn_two, wu, 1, 0)
    sigma = jax.nn.sigmoid(gate)
    silu = gate * sigma
    act = (silu * up).astype(BF)
    dact = dot(cot, wd, 1, 1)
    dgate = (dact * up * sigma * (1.0 + gate * (1.0 - sigma))).astype(BF)
    dup = (dact * silu).astype(BF)

    def reduce(piece):
        if m != 4:
            return lax.psum(piece, "ctx")
        one = (piece.astype(F32) + lax.ppermute(piece, "ctx", [(0, 1), (3, 2)]).astype(F32)).astype(BF)
        two = (one.astype(F32) + lax.ppermute(one, "ctx", [(1, 2), (2, 1)]).astype(F32)).astype(BF)
        three = lax.ppermute(two, "ctx", [(1, 0), (2, 3)])
        return jnp.where((z == 0) | (z == 3), three, two)

    def share(grad, axis):
        low = grad.astype(BF)
        return [plane(part(low, f ^ k, axis), k) for k in range(n)]

    down_parts = [reduce(p) for p in share(dot(act, cot, 0, 0), 1)]
    gate_parts = [reduce(p) for p in share(dot(xn_two, dgate, 0, 0), 0)]
    up_parts = [reduce(p) for p in share(dot(xn_two, dup, 0, 0), 0)]
    d_two = scatter(dot(dgate, wg, 1, 1) + dot(dup, wu, 1, 1))
    out_half = (hidden + scatter(dot(act, wd, 1, 0))).astype(BF)
    output = join(out_half, swap(out_half))
    gain_two_grad = jnp.sum(d_two * hat_two, 0)
    e_two = d_two * gain_two
    d_hidden = mine(cotangent[0], t).astype(F32) + scale_two * (e_two - hat_two * row_mean(e_two * hat_two))
    dhb = gather(d_hidden.astype(BF))
    out_parts = [reduce(p) for p in share(dot(attended_low, dhb, 0, 0), 1)]

    d_att = dot(dhb, wo, 1, 1).astype(BF).reshape(n, tokens, heads, HD)
    delta = jnp.einsum("nthd,nthd->nht", d_att.astype(F32), attended)
    d_weights = jnp.einsum("nthd,nsd->nhts", d_att, values, preferred_element_type=F32)
    d_scores = (weights * (d_weights - delta[..., None])).astype(BF)
    dv = jnp.einsum("nhts,nthd->nsd", weights_low, d_att, preferred_element_type=F32)
    dk = jnp.einsum("nhts,nthd->nsd", d_scores, query, preferred_element_type=F32) * factor
    dq = jnp.einsum("nhts,nsd->nthd", d_scores, keys, preferred_element_type=F32) * factor
    d_kv = jnp.concatenate([dk, dv], -1).reshape(n, m, tokens, 2 * HD)
    d_low = d_kv.astype(BF)
    d_kv_own = d_kv[:, 0]
    for k in range(1, m):
        d_kv_own = d_kv_own + column(d_low[:, k], k).astype(F32)
    d_kv_own = d_kv_own.reshape(n * tokens, 2 * HD)
    dq = rotate(dq.reshape(n * tokens, heads, HD), cosine, -sine).reshape(n * tokens, cols)
    dk = rotate(d_kv_own[:, None, :HD], cosine, -sine)[:, 0, :]
    d_qkv = jnp.concatenate([dq, dk, d_kv_own[:, HD:]], 1).astype(BF)
    w_here = jnp.concatenate([w_qkv[:, :cols], pick(w_qkv[:, cols : cols + kw]), pick(w_qkv[:, cols + kw :])], 1)
    d_one = scatter(dot(d_qkv, w_here, 1, 1))
    qkv_parts = share(dot(xn_one, d_qkv, 0, 0), 0)
    key_parts, value_parts = [0.0] * kv_heads, [0.0] * kv_heads
    for k in range(n):
        owner = (heads * (f ^ k)) // ((w_query.shape[1] // HD) // kv_heads)
        piece = qkv_parts[k].astype(F32)
        for g in range(kv_heads):
            key_parts[g] = key_parts[g] + jnp.where(owner == g, piece[:, cols : cols + HD], 0.0)
            value_parts[g] = value_parts[g] + jnp.where(owner == g, piece[:, cols + HD :], 0.0)
    small = reduce(jnp.concatenate(key_parts + value_parts, 1).astype(BF)).astype(F32)
    query_parts = [reduce(p[:, :cols]) for p in qkv_parts]
    gain_one_grad = jnp.sum(d_one * hat_one, 0)
    e_one = d_one * gain_one
    in_half = d_hidden + scale_one * (e_one - hat_one * row_mean(e_one * hat_one))
    input_grad = join(in_half, swap(in_half))
    gain_grads = jnp.stack([gain_one_grad, gain_two_grad])
    nothing = jnp.zeros_like(gain_grads)
    gain_grads = jnp.where(t == 0, jnp.concatenate([gain_grads, nothing], 1), jnp.concatenate([nothing, gain_grads], 1))
    gain_grads = part(lax.psum(gain_grads, ("fsdp", "ctx", "tp")), f, 1)

    def settle(pieces, axis):
        return place(pieces, axis).astype(F32)

    return (
        output[None],
        input_grad[None],
        gain_grads[0],
        settle(query_parts, 1),
        small[:, :kw],
        small[:, kw:],
        settle(out_parts, 0),
        gain_grads[1],
        settle(gate_parts, 1),
        settle(up_parts, 1),
        settle(down_parts, 0),
    )


T, W, H, TILE = 256, 2048, 1024, 128
MAIN, WIN = 640, 768
GRADS = (("d", 2816, 512), ("g", 512, 2816), ("u", 512, 2816), ("o", 1024, 512), ("q", 512, 1024), ("k", 512, 256))
CHUNKS = [
    (name, r, c, min(512, rows - r), min(512, cols - c))
    for name, rows, cols in GRADS
    for r in range(0, rows, 512)
    for c in range(0, cols, 512)
]
MESH = pl.DeviceIdType.MESH


def nn(a, b):
    return lax.dot_general(a, b, (((1,), (0,)), ((), ())), preferred_element_type=F32)


def nt(a, b):
    return lax.dot_general(a, b, (((1,), (1,)), ((), ())), preferred_element_type=F32)


def tn(a, b):
    return lax.dot_general(a, b, (((0,), (0,)), ((), ())), preferred_element_type=F32)


def flip(a, k):
    return (a % 2 + k % 2) % 2 + 2 * ((a // 2 + k // 2) % 2)


def layer_kernel(*refs):
    names = iter(refs)

    def take(count):
        return [next(names) for _ in range(count)]

    x_in, table_in, gains_in, cot_in, wq, wk, wv, wo, wg, wu, wd = take(11)
    out_ref, in_grad_ref, gain_ref = take(3)
    first, left, cross, total = ({name: next(names) for name, _, _ in GRADS} for _ in range(4))
    (x1, x2, ct, dh, w_qkv, w_o, w_g, w_u, w_d, act, dg, du, q_buf, kv_all, ob) = take(15)
    (ps, pr, rr, yo, hid, d_hid, xv, tb, ga, ids, r1s, r2s, ss_own, ss_other, lse, bias) = take(16)
    (gs_d, kv_g, la, lb, ring, tt, d_kv, d_kv_recv, out_s, g_sum, g_plane, g_column, g_whole) = take(13)
    send_sem, recv_sem, local_sem, credit = take(4)
    f, z, t = lax.axis_index("fsdp"), lax.axis_index("ctx"), lax.axis_index("tp")
    sems = iter(range(10**6))
    drains = []

    def al(v, by):
        return pl.multiple_of(v, by)

    def plane(k):
        return (flip(f, k), z, t)

    def column(k):
        return (f, flip(z, k), t)

    core = (f, z, 1 - t)
    rows_f = pl.ds(al(f * T, T), T)
    half = pl.ds(al(t * H, H), H)
    rest = pl.ds(al((1 - t) * H, H), H)

    def rows_of(b):
        return pl.ds(al(b * T, T), T)

    def remote(src, dst, s, device):
        return pltpu.make_async_remote_copy(src_ref=src, dst_ref=dst, send_sem=send_sem.at[s], recv_sem=recv_sem.at[s], device_id=device, device_id_type=MESH)

    def here(src, dst, s):
        return pltpu.make_async_copy(src, dst, local_sem.at[s])

    local_count = iter(range(10**6))

    lx = here(x_in.at[0], xv, next(local_count))
    lx.start()
    lc = here(cot_in.at[0], ct.at[rows_f, :], next(local_count))
    lc.start()
    lh = here(cot_in.at[0, :, half], out_s, next(local_count))
    lh.start()
    lt = here(table_in, tb.at[f], next(local_count))
    lt.start()
    lg = here(gains_in, ga.at[:, pl.ds(al(f * 512, 512), 512)], next(local_count))
    lg.start()

    def starts(r):
        return (11 * r + 1) // 2

    def weight_moves(k, s0, wait_side):
        r = flip(f, k)
        mine = f if not wait_side else r
        rows = pl.ds(al(mine * 512, 512), 512)
        begin = al(starts(r) * TILE, TILE) if not wait_side else al(starts(f) * TILE, TILE)
        tail = al(begin + MAIN, TILE)
        col = al((r if not wait_side else f) * T, T)
        return {
            "qkv": [(wq.at[:, pl.ds(col, T)], w_qkv.at[rows, pl.ds(0, T)]), (wk, w_qkv.at[rows, pl.ds(T, TILE)]), (wv, w_qkv.at[rows, pl.ds(T + TILE, TILE)])],
            "o": [(wo.at[pl.ds(col, T), :], w_o.at[:, rows])],
            "gu": [(wg.at[:, pl.ds(begin, MAIN)], w_g.at[rows, pl.ds(0, MAIN)]), (wu.at[:, pl.ds(begin, MAIN)], w_u.at[rows, pl.ds(0, MAIN)])],
            "d": [(wd.at[pl.ds(begin, MAIN), :], w_d.at[pl.ds(0, MAIN), rows])],
            "gu_tail": [(wg.at[:, pl.ds(tail, TILE)], w_g.at[rows, pl.ds(MAIN, TILE)]), (wu.at[:, pl.ds(tail, TILE)], w_u.at[rows, pl.ds(MAIN, TILE)])],
            "d_tail": [(wd.at[pl.ds(tail, TILE), :], w_d.at[pl.ds(MAIN, TILE), rows])],
        }

    w_sem = {(key, k, i): next(sems) for key, c in (("qkv", 3), ("o", 1), ("gu", 2), ("d", 1), ("gu_tail", 2), ("d_tail", 1)) for k in (1, 2, 3) for i in range(c)}
    w_local = {(key, i): next(local_count) for key, c in (("qkv", 3), ("o", 1), ("gu", 2), ("d", 1), ("gu_tail", 2), ("d_tail", 1)) for i in range(c)}

    def weights_start(key):
        for k in (1, 2, 3):
            for i, (src, dst) in enumerate(weight_moves(k, 0, False)[key]):
                remote(src, dst, w_sem[key, k, i], plane(k)).start()
            if key in ("gu", "d"):

                @pl.when(flip(f, k) % 2 == 0)
                def _():
                    for i, (src, dst) in enumerate(weight_moves(k, 0, False)[key + "_tail"]):
                        remote(src, dst, w_sem[key + "_tail", k, i], plane(k)).start()

    def weights_own(wait):
        moves = weight_moves(0, 0, False)
        for key in ("qkv", "o", "gu", "d"):
            for i, (src, dst) in enumerate(moves[key]):
                cp = here(src, dst, w_local[key, i])
                cp.wait() if wait else cp.start()

        @pl.when(f % 2 == 0)
        def _():
            for key in ("gu_tail", "d_tail"):
                for i, (src, dst) in enumerate(moves[key]):
                    cp = here(src, dst, w_local[key, i])
                    cp.wait() if wait else cp.start()

    def weights_wait(key):
        for k in (1, 2, 3):
            for i, (src, dst) in enumerate(weight_moves(k, 0, True)[key]):
                remote(src, dst, w_sem[key, k, i], plane(k)).wait_recv()
            if key in ("gu", "d"):

                @pl.when(f % 2 == 0)
                def _():
                    for i, (src, dst) in enumerate(weight_moves(k, 0, True)[key + "_tail"]):
                        remote(src, dst, w_sem[key + "_tail", k, i], plane(k)).wait_recv()

    def weights_drain():
        for key in ("qkv", "o", "gu", "d"):
            for k in (1, 2, 3):
                for i, (src, dst) in enumerate(weight_moves(k, 0, False)[key]):
                    remote(src, dst, w_sem[key, k, i], plane(k)).wait_send()
                if key in ("gu", "d"):

                    @pl.when(flip(f, k) % 2 == 0)
                    def _():
                        for i, (src, dst) in enumerate(weight_moves(k, 0, False)[key + "_tail"]):
                            remote(src, dst, w_sem[key + "_tail", k, i], plane(k)).wait_send()

    g_sem = [[next(sems) for _ in range(3)] for _ in range(4)]
    f_sem = [[next(sems) for _ in range(4)] for _ in range(4)]

    def gather_start(g, buf, with_own, src=None):
        block = buf.at[rows_f, half]
        for k in (1, 2, 3):
            remote(block if src is None else src, block, g_sem[g][k - 1], plane(k)).start()
        if with_own:
            remote(block, block, f_sem[g][3], core).start()

    def gather_forward(g, buf):
        for k in (1, 2, 3):
            block = buf.at[rows_of(flip(f, k)), half]
            remote(block, block, g_sem[g][k - 1], plane(k)).wait_recv()
            remote(block, block, f_sem[g][k - 1], core).start()

    def gather_take(g, buf, k):
        if k == 0:
            block = buf.at[rows_f, rest]
            remote(block, block, f_sem[g][3], core).wait_recv()
        else:
            block = buf.at[rows_of(flip(f, k)), rest]
            remote(block, block, f_sem[g][k - 1], core).wait_recv()

    def gather_drain(g, buf, with_own, src=None):
        block = buf.at[rows_f, half]
        for k in (1, 2, 3):
            remote(block if src is None else src, block, g_sem[g][k - 1], plane(k)).wait_send()
            other = buf.at[rows_of(flip(f, k)), half]
            remote(other, other, f_sem[g][k - 1], core).wait_send()
        if with_own:
            remote(block, block, f_sem[g][3], core).wait_send()

    t_sem = [next(sems) for _ in range(3)]
    a_sem = [next(sems) for _ in range(3)]
    own_gain = ga.at[:, pl.ds(al(f * 512, 512), 512)]

    barrier = pltpu.get_barrier_semaphore()
    for k in (1, 2, 3):
        pl.semaphore_signal(barrier, inc=1, device_id=plane(k), device_id_type=MESH)
        pl.semaphore_signal(barrier, inc=1, device_id=column(k), device_id_type=MESH)
    pl.semaphore_signal(barrier, inc=1, device_id=core, device_id_type=MESH)
    pl.semaphore_wait(barrier, 7)

    lt.wait()
    lg.wait()
    for k in (1, 2, 3):
        remote(own_gain, own_gain, a_sem[k - 1], plane(k)).start()
        remote(tb.at[f], tb.at[f], t_sem[k - 1], plane(k)).start()
    weights_start("qkv")
    weights_own(False)

    @pl.when(f % 2 == 1)
    def _():
        w_g[:, MAIN:WIN] = jnp.zeros((W, TILE), BF)
        w_u[:, MAIN:WIN] = jnp.zeros((W, TILE), BF)
        w_d[MAIN:WIN, :] = jnp.zeros((TILE, W), BF)

    lx.wait()
    for k in (1, 2, 3):
        dst = ga.at[:, pl.ds(al(flip(f, k) * 512, 512), 512)]
        remote(dst, dst, a_sem[k - 1], plane(k)).wait_recv()

    STEP = 32

    def sub(i):
        return pl.ds(al(i * STEP, STEP), STEP)

    @pl.loop(0, T // STEP)
    def _(i):
        xs = xv[sub(i), :].astype(F32)
        scale = lax.rsqrt(jnp.mean(xs * xs, axis=-1, keepdims=True) + EPSILON)
        r1s[sub(i), :] = jnp.broadcast_to(scale, (STEP, TILE))
        x1[pl.ds(al(f * T + i * STEP, STEP), STEP), :] = (xs * scale * ga[0:1, :]).astype(BF)

    gather_start(0, x1, False)
    weights_start("o")
    for k in (1, 2, 3):
        dst = tb.at[flip(f, k)]
        remote(dst, dst, t_sem[k - 1], plane(k)).wait_recv()
    weights_own(True)
    weights_wait("qkv")
    weights_start("gu")

    lane = lax.broadcasted_iota(jnp.int32, (T, TILE), 1)
    low_lane = lane < HD
    first_half = lane % HD < HD // 2
    kv_head = f // 2

    def turns(b):
        cosine, sine = tb[b, 0:32, :], tb[b, 32:64, :]
        return (
            jnp.transpose(jnp.concatenate([cosine] * 4, 0)),
            jnp.transpose(jnp.concatenate([-sine, sine, -sine, sine], 0)),
        )

    def turn(v, c, s):
        swapped = jnp.where(first_half, pltpu.roll(v, TILE - 32, 1), pltpu.roll(v, 32, 1))
        return v * c + swapped * s

    def qkv_block(k):
        b = flip(f, k)
        qkv = nn(x1[rows_of(b), :], w_qkv[...])
        c, s = turns(b)
        for i in range(2):
            q = turn(qkv[:, i * TILE : (i + 1) * TILE], c, s) * 0.125
            q_buf[rows_of(b), i * TILE : (i + 1) * TILE] = q.astype(BF)
        key = turn(qkv[:, 2 * TILE : 3 * TILE], c, s)
        value = qkv[:, 3 * TILE :]
        key = jnp.where(kv_head == 0, key, pltpu.roll(key, HD, 1))
        value = jnp.where(kv_head == 1, value, pltpu.roll(value, HD, 1))
        kv_all[z, b, :, :] = jnp.where(low_lane, key, value).astype(BF)
        ids[z, pl.ds(b, 1), :] = tb[b, 64:65, :]

    qkv_block(0)
    gather_forward(0, x1)
    for k in (1, 2, 3):
        gather_take(0, x1, k)

    @pl.loop(1, 4)
    def _(k):
        qkv_block(k)

    z_sem = [[next(sems) for _ in range(2)] for _ in range(3)]
    for k in (1, 2, 3):
        remote(kv_all.at[z], kv_all.at[z], z_sem[k - 1][0], column(k)).start()
        remote(ids.at[z], ids.at[z], z_sem[k - 1][1], column(k)).start()
    gather_start(1, ct, False, cot_in.at[0, :, half])
    for k in (1, 2, 3):
        zz = flip(z, k)
        remote(kv_all.at[zz], kv_all.at[zz], z_sem[k - 1][0], column(k)).wait_recv()
        remote(ids.at[zz], ids.at[zz], z_sem[k - 1][1], column(k)).wait_recv()
    lc.wait()

    low_keys = lax.broadcasted_iota(jnp.int32, (4 * T, TILE), 1) < HD

    def bias_of(s):
        query_id = ids[z, pl.ds(s, 1), :]
        for j in range(4):
            key_id = jnp.transpose(jnp.broadcast_to(ids[j, pl.ds(s, 1), :], (8, T)))[:, 0:1]
            bias[j * T : (j + 1) * T, :] = jnp.where(key_id <= query_id, 0.0, NEGATIVE).astype(BF)

    def kv_of(s):
        kv = jnp.concatenate([kv_all[j, s, :, :] for j in range(4)], 0).astype(F32)
        turned = pltpu.roll(kv, HD, 1)
        keys = jnp.where(low_keys, kv, turned).astype(BF)
        values = jnp.where(low_keys, turned, kv).astype(BF)
        return kv, keys, values

    def only(v, parity):
        return jnp.where(low_lane if parity == 0 else ~low_lane, v.astype(F32), 0.0).astype(BF)

    @pl.loop(0, 4)
    def _(s):
        bias_of(s)
        kv, keys, _ = kv_of(s)
        values_t = jnp.transpose(kv)[HD:, :].astype(BF)

        for i in range(2):
            mixed = []
            for parity in range(2):
                q = only(q_buf[rows_of(s), i * TILE : (i + 1) * TILE], parity)
                scores = nt(keys, q) + bias[...].astype(F32)
                top = jnp.max(scores, axis=0, keepdims=True)
                raw = jnp.exp(scores - top)
                norm = jnp.sum(raw, axis=0, keepdims=True)
                lse[s, 2 * i + parity : 2 * i + parity + 1, :] = top + jnp.log(norm)
                weights = (raw * (1.0 / norm)).astype(BF)
                mixed.append(nn(values_t, weights))
            ob[rows_of(s), i * TILE : (i + 1) * TILE] = jnp.transpose(jnp.concatenate(mixed, 0)).astype(BF)

    p_sem = [[next(sems) for _ in range(4)] for _ in range(4)]
    s_sem = [[next(sems) for _ in range(3)] for _ in range(4)]
    COLS = 256

    def scatter_start(u, product):
        p0, s0 = p_sem[u][0], s_sem[u][0]

        @pl.loop(0, 4)
        def _(i):
            k = (i + 1) % 4
            b = flip(f, k)

            @pl.loop(0, H // COLS)
            def _(j):
                ps[k, :, pl.ds(al(j * COLS, COLS), COLS)] = product(b, (1 - t) * H + j * COLS).astype(BF)

            remote(ps.at[k], pr.at[k], p0 + k, core).start()

        def own(k, j):
            b = flip(f, k)
            cols = pl.ds(al(j * COLS, COLS), COLS)
            return product(b, t * H + j * COLS) + pr[k, :, cols].astype(F32)

        @pl.loop(1, 4)
        def _(k):
            remote(ps.at[k], pr.at[k], p0 + k, core).wait()

            @pl.loop(0, H // COLS)
            def _(j):
                ps[k, :, pl.ds(al(j * COLS, COLS), COLS)] = own(k, j).astype(BF)

            remote(ps.at[k], rr.at[k - 1], s0 + k - 1, plane(k)).start()

        remote(ps.at[0], pr.at[0], p0, core).wait()

        @pl.loop(0, H // COLS)
        def _(j):
            yo[:, pl.ds(al(j * COLS, COLS), COLS)] = own(0, j)

    def scatter_wait(u):
        for k in (1, 2, 3):
            remote(ps.at[k], rr.at[k - 1], s_sem[u][k - 1], plane(k)).wait()

    def scattered(i):
        return yo[sub(i), :] + rr[0, sub(i), :].astype(F32) + rr[1, sub(i), :].astype(F32) + rr[2, sub(i), :].astype(F32)

    n_sem = [next(sems) for _ in range(3)]

    def core_sums(u):
        remote(ss_own.at[u], ss_other.at[u], n_sem[u], core).start()
        remote(ss_own.at[u], ss_other.at[u], n_sem[u], core).wait()

    weights_wait("o")
    weights_wait("gu")
    weights_start("d")
    scatter_start(0, lambda b, c: nn(ob[rows_of(b), :], w_o[:, pl.ds(al(c, COLS), COLS)]))
    scatter_wait(0)

    @pl.loop(0, T // STEP)
    def _(i):
        rows = xv[sub(i), half].astype(F32) + scattered(i)
        hid[sub(i), :] = rows
        ss_own[0, sub(i), :] = jnp.broadcast_to(jnp.sum(rows * rows, axis=-1, keepdims=True), (STEP, TILE))

    core_sums(0)
    gain_one, gain_two = ga[0:1, half], ga[1:2, half]

    @pl.loop(0, T // STEP)
    def _(i):
        scale = lax.rsqrt((ss_own[0, sub(i), 0:1] + ss_other[0, sub(i), 0:1]) * (1.0 / W) + EPSILON)
        r2s[sub(i), :] = jnp.broadcast_to(scale, (STEP, TILE))
        x2[pl.ds(al(f * T + i * STEP, STEP), STEP), half] = (hid[sub(i), :] * scale * gain_two).astype(BF)

    gather_start(2, x2, True)
    gather_forward(1, ct)
    for k in (1, 2, 3):
        gather_take(1, ct, k)
    weights_wait("d")
    gather_forward(2, x2)
    gather_take(2, x2, 0)

    UNITS = 256

    def feed_block(k):
        b = flip(f, k)

        @pl.loop(0, WIN // UNITS)
        def _(j):
            cols = pl.ds(al(j * UNITS, UNITS), UNITS)
            gate = nn(x2[rows_of(b), :], w_g[:, cols])
            up = nn(x2[rows_of(b), :], w_u[:, cols])
            back = nt(ct[rows_of(b), :], w_d[cols, :])
            sigma = jax.nn.sigmoid(gate)
            silu = gate * sigma
            act[rows_of(b), cols] = (silu * up).astype(BF)
            dg[rows_of(b), cols] = (back * up * sigma * (1.0 + gate * (1.0 - sigma))).astype(BF)
            du[rows_of(b), cols] = (back * silu).astype(BF)

    feed_block(0)
    for k in (1, 2, 3):
        gather_take(2, x2, k)

    @pl.loop(1, 4)
    def _(k):
        feed_block(k)

    e_sem = {(name, k, i): next(sems) for name in "dguoqk" for k in (1, 2, 3) for i in range(2)}
    e_local = {(name, i): next(local_count) for name in "dguoqk" for i in range(2)}
    mine = al(starts(f) * TILE, TILE)

    def stage(name, k):
        if name == "d":
            return gs_d.at[pl.ds(k * WIN, WIN), :]
        if name in "gu":
            return ct.at[pl.ds((k // 2) * 512, 512), pl.ds((k % 2) * H, WIN)]
        if name == "o":
            return gs_d.at[pl.ds(k * WIN, T), :]
        return x2.at[pl.ds((k // 2) * 512, 512), pl.ds((k % 2) * 512 + (0 if name == "q" else T), T)]

    def grad_moves(name, k, sender):
        buf, begin = stage(name, k), al(starts(sender) * TILE, TILE)
        tail = al(begin + MAIN, TILE)
        if name == "d":
            return [(buf.at[pl.ds(0, MAIN), :], first["d"].at[pl.ds(begin, MAIN), :]), (buf.at[pl.ds(MAIN, TILE), :], first["d"].at[pl.ds(tail, TILE), :])]
        if name in "gu":
            return [(buf.at[:, pl.ds(0, MAIN)], first[name].at[:, pl.ds(begin, MAIN)]), (buf.at[:, pl.ds(MAIN, TILE)], first[name].at[:, pl.ds(tail, TILE)])]
        if name == "o":
            return [(buf, first["o"].at[rows_of(sender), :])]
        if name == "q":
            return [(buf, first["q"].at[:, rows_of(sender)])]
        return [(buf, kv_g.at[k - 1])]

    def grad_send(name, k, act_on, only_wait=False):
        for i, (src, dst) in enumerate(grad_moves(name, k, f)):

            def run(i=i, src=src, dst=dst):
                if k == 0:
                    cp = here(src, dst, e_local[name, i])
                    cp.wait() if act_on == "wait" else cp.start()
                else:
                    cp = remote(src, dst, e_sem[name, k, i], plane(k))
                    cp.wait_send() if act_on == "wait" else cp.start()

            if i == 0:
                run()
            else:
                pl.when(f % 2 == 0)(run)

    def grad_take(name):
        for k in (1, 2, 3):
            sender = flip(f, k)
            for i, (src, dst) in enumerate(grad_moves(name, k, sender)):

                def run(i=i, src=src, dst=dst):
                    remote(src, dst, e_sem[name, k, i], plane(k)).wait_recv()

                if i == 0:
                    run()
                else:
                    pl.when(sender % 2 == 0)(run)

    def block_cols(k):
        return pl.ds(al(flip(f, k) * 512, 512), 512)

    for k in (1, 2, 3, 0):

        @pl.loop(0, WIN // UNITS)
        def _(j):
            cols = pl.ds(al(j * UNITS, UNITS), UNITS)
            gs_d[pl.ds(al(k * WIN + j * UNITS, UNITS), UNITS), :] = tn(act[:, cols], ct[:, block_cols(k)]).astype(BF)

        grad_send("d", k, "start")

    scatter_start(1, lambda b, c: nt(dg[rows_of(b), :], w_g[pl.ds(al(c, COLS), COLS), :]) + nt(du[rows_of(b), :], w_u[pl.ds(al(c, COLS), COLS), :]))

    gather_drain(1, ct, False, cot_in.at[0, :, half])
    def feed_grads(name, right):
        for k in (1, 2, 3, 0):

            @pl.loop(0, 2)
            def _(i):
                xs = x2[:, pl.ds(al(flip(f, k) * 512 + i * T, T), T)]
                stage(name, k)[pl.ds(al(i * T, T), T), :] = tn(xs, right[...]).astype(BF)

            grad_send(name, k, "start")

    feed_grads("g", dg)

    end = (z == 0) | (z == 3)
    middle = (z == 1) | (z == 2)
    next_in = (f, jnp.where(z < 2, 1, 2), t)
    next_out = (f, jnp.where(z < 2, 0, 3), t)
    facing = (f, 3 - z, t)
    l_sem = [[next(sems) for _ in range(3)] for _ in CHUNKS]
    v_sem = [next(local_count) for _ in range(2)]
    o_sem = [next(local_count) for _ in CHUNKS]
    DEPTH = 2

    def window(arrays, i):
        name, r, c, rows, cols = CHUNKS[i]
        return arrays[name].at[pl.ds(r, rows), pl.ds(c, cols)]

    def line_send(name):
        @pl.when(end)
        def _():
            for i, chunk in enumerate(CHUNKS):
                if chunk[0] == name:
                    remote(window(first, i), window(left, i), l_sem[i][0], next_in).start()

    def add_into(dst, a, b, rows, cols):
        @pl.loop(0, rows // STEP)
        def _(i):
            at = sub(i)
            dst[at, pl.ds(0, cols)] = (a[at, pl.ds(0, cols)].astype(F32) + b[at, pl.ds(0, cols)].astype(F32)).astype(BF)

    def line_one(i):
        name, r, c, rows, cols = CHUNKS[i]
        part = (pl.ds(0, rows), pl.ds(0, cols))
        a, b, keep = la.at[part], lb.at[part], ring.at[i % DEPTH]

        @pl.when(middle)
        def _():
            get_a = here(window(first, i), a, v_sem[0])
            get_a.start()
            remote(window(first, i), window(left, i), l_sem[i][0], next_in).wait_recv()
            get_b = here(window(left, i), b, v_sem[1])
            get_b.start()
            get_a.wait()
            get_b.wait()
            add_into(keep, la, lb, rows, cols)
            remote(keep.at[part], window(cross, i), l_sem[i][1], facing).start()

    def line_two(i):
        name, r, c, rows, cols = CHUNKS[i]
        part = (pl.ds(0, rows), pl.ds(0, cols))
        keep, done = ring.at[i % DEPTH], tt.at[i % 2]

        @pl.when(middle)
        def _():
            remote(keep.at[part], window(cross, i), l_sem[i][1], facing).wait()
            get = here(window(cross, i), lb.at[part], v_sem[1])
            get.start()
            if i >= 2:
                line_out(i - 2)
            get.wait()
            add_into(done, keep, lb, rows, cols)
            remote(done.at[part], window(total, i), l_sem[i][2], next_out).start()
            here(done.at[part], window(total, i), o_sem[i]).start()

    def line_out(i):
        name, r, c, rows, cols = CHUNKS[i]
        done = tt.at[i % 2].at[pl.ds(0, rows), pl.ds(0, cols)]
        remote(done, window(total, i), l_sem[i][2], next_out).wait_send()
        here(done, window(total, i), o_sem[i]).wait()

    pumped = [0]

    def pump(name):
        while pumped[0] < len(CHUNKS) and CHUNKS[pumped[0]][0] == name:
            i = pumped[0]
            line_one(i)
            if i >= 1:
                line_two(i - 1)
            pumped[0] += 1

    def grad_ready(name):
        grad_take(name)
        grad_send(name, 0, "wait")
        line_send(name)

    grad_ready("d")
    scatter_wait(1)

    lh.wait()

    def norm_two_back(i, carry):
        rows = scattered(i)
        yo[sub(i), :] = rows
        hat = hid[sub(i), :] * r2s[sub(i), 0:1]
        ss_own[1, sub(i), :] = jnp.broadcast_to(jnp.sum(rows * gain_two * hat, axis=-1, keepdims=True), (STEP, TILE))
        return carry + jnp.sum(rows * hat, axis=0, keepdims=True)

    g_sum[...] = jnp.zeros((8, H), F32)
    g_sum[1:2, :] = lax.fori_loop(0, T // STEP, norm_two_back, jnp.zeros((1, H), F32))
    core_sums(1)

    @pl.loop(0, T // STEP)
    def _(i):
        scale = r2s[sub(i), 0:1]
        hat = hid[sub(i), :] * scale
        mean = (ss_own[1, sub(i), 0:1] + ss_other[1, sub(i), 0:1]) * (1.0 / W)
        rows = out_s[sub(i), :].astype(F32) + scale * (yo[sub(i), :] * gain_two - hat * mean)
        d_hid[sub(i), :] = rows
        dh[pl.ds(al(f * T + i * STEP, STEP), STEP), half] = rows.astype(BF)

    gather_start(3, dh, True)
    grad_ready("g")
    gather_forward(3, dh)
    pump("d")
    for k in range(4):
        gather_take(3, dh, k)
    for k in (1, 2, 3):
        grad_send("g", k, "wait")
    feed_grads("u", du)

    for k in (1, 2, 3):
        grad_send("d", k, "wait")
    for k in (1, 2, 3, 0):
        gs_d[k * WIN : k * WIN + T, :] = tn(ob[...], dh[:, block_cols(k)]).astype(BF)
        grad_send("o", k, "start")

    @pl.loop(0, 4)
    def _(b):
        ob[rows_of(b), :] = nt(dh[rows_of(b), :], w_o[...]).astype(BF)

    d_ob, d_qkv = ob, dg
    scatter_start(2, lambda b, c: nn(act[rows_of(b), :], w_d[:, pl.ds(al(c, COLS), COLS)]))

    gather_drain(2, x2, True)

    def attend_back(s):
        bias_of(s)
        kv, keys, values = kv_of(s)
        keys_t = jnp.transpose(kv)[:HD, :].astype(BF)
        c, sn = turns(s)
        d_key = jnp.zeros((4 * T, TILE), F32)
        d_value = jnp.zeros((4 * T, TILE), F32)
        for i in range(2):
            d_query = []
            for parity in range(2):
                q = only(q_buf[rows_of(s), i * TILE : (i + 1) * TILE], parity)
                do = only(d_ob[rows_of(s), i * TILE : (i + 1) * TILE], parity)
                weights = jnp.exp(nt(keys, q) + bias[...].astype(F32) - lse[s, 2 * i + parity : 2 * i + parity + 1, :])
                d_weights = nt(values, do)
                delta = jnp.sum(weights * d_weights, axis=0, keepdims=True)
                d_scores = (weights * (d_weights - delta)).astype(BF)
                d_value = d_value + nn(weights.astype(BF), do)
                d_key = d_key + nn(d_scores, q)
                d_query.append(nn(keys_t, d_scores))
            d_query = jnp.transpose(jnp.concatenate(d_query, 0)) * 0.125
            d_qkv[rows_of(s), i * TILE : (i + 1) * TILE] = turn(d_query, c, -sn).astype(BF)
        d_key = d_key + pltpu.roll(d_key, HD, 1)
        d_value = d_value + pltpu.roll(d_value, HD, 1)
        both = jnp.where(low_keys, d_key, d_value)
        own = both[0:T, :]
        for j in range(1, 4):
            own = jnp.where(z == j, both[j * T : (j + 1) * T, :], own)
        d_kv[s, :, :] = own
        for j in range(4):
            x2[rows_of(s), H + j * TILE : H + (j + 1) * TILE] = both[j * T : (j + 1) * T, :].astype(BF)

    @pl.loop(0, 2)
    def _(s):
        attend_back(s)

    grad_ready("u")
    pump("g")
    scatter_wait(2)

    @pl.loop(0, T // STEP)
    def _(i):
        out_s[sub(i), :] = (hid[sub(i), :] + scattered(i)).astype(BF)

    for k in (1, 2, 3):
        pl.semaphore_signal(credit, inc=1, device_id=plane(k), device_id_type=MESH)
    pl.semaphore_signal(credit, inc=1, device_id=core, device_id_type=MESH)
    out_local = here(out_s, out_ref.at[:, half], next(local_count))
    out_local.start()
    out_remote = remote(out_s, out_ref.at[:, half], next(sems), core)
    out_remote.start()

    @pl.loop(2, 4)
    def _(s):
        attend_back(s)

    k_sem = [next(sems) for _ in range(3)]
    for k in (1, 2, 3):
        remote(x2.at[:, pl.ds(al(H + flip(z, k) * TILE, TILE), TILE)], d_kv_recv.at[k - 1], k_sem[k - 1], column(k)).start()
    grad_ready("o")
    pump("u")
    for k in (1, 2, 3):
        remote(x2.at[:, pl.ds(al(H + flip(z, k) * TILE, TILE), TILE)], d_kv_recv.at[k - 1], k_sem[k - 1], column(k)).wait()

    here_half = low_lane if False else (lane // HD) == kv_head

    @pl.loop(0, 4)
    def _(s):
        c, sn = turns(s)
        whole = d_kv[s, :, :]
        for k in range(3):
            whole = whole + d_kv_recv[k, rows_of(s), :].astype(F32)
        turned = pltpu.roll(whole, HD, 1)
        d_key = turn(jnp.where(low_lane, whole, turned), c, -sn)
        d_value = jnp.where(low_lane, turned, whole)
        d_qkv[rows_of(s), 2 * TILE : 3 * TILE] = jnp.where(here_half, d_key, 0.0).astype(BF)
        d_qkv[rows_of(s), 3 * TILE : 4 * TILE] = jnp.where(here_half, d_value, 0.0).astype(BF)

    for k in (1, 2, 3, 0):

        @pl.loop(0, 2)
        def _(i):
            xs = x1[:, pl.ds(al(flip(f, k) * 512 + i * T, T), T)]
            x2[pl.ds(al((k // 2) * 512 + i * T, T), T), (k % 2) * 512 : (k % 2) * 512 + 512] = tn(xs, d_qkv[:, 0:512]).astype(BF)

        grad_send("q", k, "start")
        if k:
            grad_send("k", k, "start")
    pl.semaphore_wait(credit, 4)
    scatter_start(3, lambda b, c: nt(d_qkv[rows_of(b), 0:512], w_qkv[pl.ds(al(c, COLS), COLS), :]))
    pump("o")
    grad_ready("q")
    grad_take("k")

    @pl.loop(0, 512 // STEP)
    def _(i):
        rows = x2[sub(i), T : 2 * T].astype(F32)
        for k in (1, 2, 3):
            rows = rows + kv_g[k - 1, sub(i), :].astype(F32)
        la[sub(i), 0:T] = rows.astype(BF)

    kv_copy = here(la.at[:, pl.ds(0, T)], first["k"], next(local_count))
    kv_copy.start()
    kv_copy.wait()
    line_send("k")
    pump("q")
    scatter_wait(3)

    def norm_one_back(i, carry):
        rows = scattered(i)
        yo[sub(i), :] = rows
        hat = xv[sub(i), half].astype(F32) * r1s[sub(i), 0:1]
        ss_own[2, sub(i), :] = jnp.broadcast_to(jnp.sum(rows * gain_one * hat, axis=-1, keepdims=True), (STEP, TILE))
        return carry + jnp.sum(rows * hat, axis=0, keepdims=True)

    g_sum[0:1, :] = lax.fori_loop(0, T // STEP, norm_one_back, jnp.zeros((1, H), F32))
    core_sums(2)

    q_sem = [[next(sems) for _ in range(3)] for _ in range(2)]
    g_plane[f, :, :] = g_sum[...]
    for k in (1, 2, 3):
        remote(g_sum, g_plane.at[f], q_sem[0][k - 1], plane(k)).start()

    @pl.loop(0, T // STEP)
    def _(i):
        scale = r1s[sub(i), 0:1]
        hat = xv[sub(i), half].astype(F32) * scale
        mean = (ss_own[2, sub(i), 0:1] + ss_other[2, sub(i), 0:1]) * (1.0 / W)
        yo[sub(i), :] = d_hid[sub(i), :] + scale * (yo[sub(i), :] * gain_one - hat * mean)

    in_local = here(yo, in_grad_ref.at[:, half], next(local_count))
    in_local.start()
    in_remote = remote(yo, in_grad_ref.at[:, half], next(sems), core)
    in_remote.start()
    for k in (1, 2, 3):
        remote(g_sum, g_plane.at[flip(f, k)], q_sem[0][k - 1], plane(k)).wait_recv()
    g_column[z, :, :] = ((g_plane[0, :, :] + g_plane[1, :, :]) + g_plane[2, :, :]) + g_plane[3, :, :]
    for k in (1, 2, 3):
        remote(g_column.at[z], g_column.at[z], q_sem[1][k - 1], column(k)).start()
    pump("k")
    line_two(len(CHUNKS) - 1)
    for k in (1, 2, 3):
        remote(g_column.at[z], g_column.at[flip(z, k)], q_sem[1][k - 1], column(k)).wait_recv()
    g_whole[:, half] = ((g_column[0, :, :] + g_column[1, :, :]) + g_column[2, :, :]) + g_column[3, :, :]
    w_move = remote(g_whole.at[:, half], g_whole.at[:, half], next(sems), core)
    w_move.start()
    w_move.wait()
    gain_move = here(g_whole.at[:, pl.ds(al(f * 512, 512), 512)], gain_ref, next(local_count))
    gain_move.start()

    @pl.when(middle)
    def _():
        line_out(len(CHUNKS) - 2)
        line_out(len(CHUNKS) - 1)

    @pl.when(end)
    def _():
        for i in range(len(CHUNKS)):
            remote(window(first, i), window(left, i), l_sem[i][0], next_in).wait_send()
            remote(window(total, i), window(total, i), l_sem[i][2], next_in).wait_recv()

    gain_move.wait()
    out_local.wait()
    out_remote.wait()
    in_local.wait()
    in_remote.wait()
    weights_drain()
    gather_drain(0, x1, False)
    gather_drain(3, dh, True)
    for k in (1, 2, 3):
        remote(own_gain, own_gain, a_sem[k - 1], plane(k)).wait_send()
        remote(tb.at[f], tb.at[f], t_sem[k - 1], plane(k)).wait_send()
        remote(kv_all.at[z], kv_all.at[z], z_sem[k - 1][0], column(k)).wait_send()
        remote(ids.at[z], ids.at[z], z_sem[k - 1][1], column(k)).wait_send()
        remote(g_sum, g_plane.at[f], q_sem[0][k - 1], plane(k)).wait_send()
        remote(g_column.at[z], g_column.at[z], q_sem[1][k - 1], column(k)).wait_send()
        for name in "uoqk":
            grad_send(name, k, "wait")
    assert next(sems) <= REMOTE_SEMS and next(local_count) <= LOCAL_SEMS


REMOTE_SEMS, LOCAL_SEMS = 400, 96


def layer_call(inputs, positions, blocks, cotangent, attn_gain, w_query, w_key, w_value, w_out, mlp_gain, w_gate, w_up, w_down):
    frequency = jnp.exp(jnp.arange(HD // 2, dtype=F32) * (-2.0 * math.log(10000.0) / HD))
    turned = frequency[:, None] * positions.astype(F32)
    table = jnp.concatenate([jnp.cos(turned), jnp.sin(turned), jnp.broadcast_to(blocks.astype(F32), (8, T))], 0)
    gains = jnp.concatenate([attn_gain[None], mlp_gain[None], jnp.zeros((6, 512), BF)], 0).astype(F32)
    shape = jax.ShapeDtypeStruct
    grads = [shape((rows, cols), BF) for _, rows, cols in GRADS]
    any_spec = pl.BlockSpec(memory_space=pl.ANY)
    v = pltpu.VMEM
    results = pl.pallas_call(
        layer_kernel,
        out_shape=[shape((T, W), BF), shape((T, W), F32), shape((8, 512), F32)] + grads * 4,
        in_specs=[any_spec] * 11,
        out_specs=[any_spec] * 27,
        scratch_shapes=[
            v((4 * T, W), BF), v((4 * T, W), BF), v((4 * T, W), BF), v((4 * T, W), BF),
            v((W, 512), BF), v((T, W), BF), v((W, WIN), BF), v((W, WIN), BF), v((WIN, W), BF),
            v((4 * T, WIN), BF), v((4 * T, WIN), BF), v((4 * T, WIN), BF),
            v((4 * T, T), BF), v((4, 4, T, TILE), BF), v((4 * T, T), BF),
            v((4, T, H), BF), v((4, T, H), BF), v((3, T, H), BF), v((T, H), F32), v((T, H), F32), v((T, H), F32), v((T, W), BF),
            v((4, 72, T), F32), v((8, W), F32), v((4, 8, T), F32), v((T, TILE), F32), v((T, TILE), F32),
            v((3, T, TILE), F32), v((3, T, TILE), F32), v((4, 8, T), F32), v((4 * T, T), BF),
            v((4 * WIN, 512), BF), v((3, 512, T), BF), v((512, 512), BF), v((512, 512), BF),
            v((2, 512, 512), BF), v((2, 512, 512), BF), v((4, T, TILE), F32), v((3, 4 * T, TILE), BF),
            v((T, H), BF), v((8, H), F32), v((4, 8, H), F32), v((4, 8, H), F32), v((8, W), F32),
            pltpu.SemaphoreType.DMA((REMOTE_SEMS,)), pltpu.SemaphoreType.DMA((REMOTE_SEMS,)),
            pltpu.SemaphoreType.DMA((LOCAL_SEMS,)), pltpu.SemaphoreType.REGULAR,
        ],
        compiler_params=pltpu.CompilerParams(collective_id=0, has_side_effects=True, vmem_limit_bytes=62 << 20),
    )(inputs, table, gains, cotangent, w_query, w_key, w_value, w_out, w_gate, w_up, w_down)
    output, input_grad, gain_grads = results[:3]
    down, gate, up, out, query, kv = (r.astype(F32) for r in results[-6:])
    return (output[None], input_grad[None], gain_grads[0], query, kv[:, :TILE], kv[:, TILE:], out, gain_grads[1], gate, up, down)


def solution(mesh):
    n, m = mesh.shape["fsdp"], mesh.shape["ctx"]

    def step(*args):
        return layer_call(*args) if n == m == 4 else local(n, m, *args)

    return jax.shard_map(
        step,
        mesh=mesh,
        in_specs=(
            P("fsdp", "ctx", None),
            P("fsdp", "ctx"),
            P("fsdp", "ctx"),
            P("fsdp", "ctx", None),
            P("fsdp"),
            P("fsdp", "tp"),
            P("fsdp", "tp"),
            P("fsdp", "tp"),
            P("tp", "fsdp"),
            P("fsdp"),
            P("fsdp", "tp"),
            P("fsdp", "tp"),
            P("tp", "fsdp"),
        ),
        out_specs=(
            P("fsdp", "ctx", None),
            P("fsdp", "ctx", None),
            P("fsdp"),
            P("fsdp", "tp"),
            P("fsdp", "tp"),
            P("fsdp", "tp"),
            P("tp", "fsdp"),
            P("fsdp"),
            P("fsdp", "tp"),
            P("fsdp", "tp"),
            P("tp", "fsdp"),
        ),
        check_vma=False,
    )
```

time: 1590 us -> 722 us (0.45)
  waiting for transfers between devices: 1230 us -> 0 us
  Pallas kernels: 0 us -> 694 us
  matrix products: 157 us -> 0 us
  blocking collectives: 102 us -> 0 us
  other arithmetic: 46.7 us -> 16.7 us
    pallas_call x0 -> x1, Pallas kernels: none -> 694 us  [layer_call(): pl.pallas_call(layer_kernel, out_shape=[shape((T, W), BF), shape((T, W),...]
    reduce_scatter x9 -> x0, waiting for transfers between devices: 498 us -> none  [the longest x1 115 us: local(): lax.psum_scatter(gate_grad.astype(jnp.bfloat16), 'fsdp', scatter_dimensio...]
    psum x4 -> x0, waiting for transfers between devices: 403 us -> none  [the longest x1 353 us: local(): lax.psum(shares[4].astype(jnp.bfloat16), 'ctx').astype(jnp.float32)]
    all_gather x5 -> x0, waiting for transfers between devices: 326 us -> none  [the longest x1 114 us: local(): lax.all_gather(w_gate, 'fsdp', axis=0, tiled=True)]
    dot_general x35 -> x0, matrix products: 157 us -> none  [the longest x4 14.3 us: masked_scores(): jnp.einsum('tkgd,skd->kgts', query_four, key_block, preferred_element_typ...]
    all_gather x7 -> x0, blocking collectives: 79.8 us -> none  [the longest x1 14.4 us: local(): lax.all_gather(value_low, 'ctx', axis=0, tiled=True)]
    reduce_sum x6 -> x0, other arithmetic: 16.5 us -> none  [the longest x2 9.25 us: stats_step(): jnp.sum(fresh, axis=-1)]
  transfers between devices with their start and end apart: 18 -> 0, of which waited for: 15 -> 0; matrix products, arithmetic and copies ran while one was open for 8% -> 0% of each run, Pallas kernels for 0% -> 0%
where the time goes in v1:
time: 722 us; the launch traced here: 720 us
  Pallas kernels  694 us (96%)
  other arithmetic  16.7 us (2%)
  local copies, waits for them, and re-layouts  7.95 us (1%)
    pallas_call x1, Pallas kernels, layer_call(): pl.pallas_call(layer_kernel, out_shape=[shape((T, W), BF), shape((T, W),...  694 us

profile of v1, /device:TPU:0, one launch (start us, length us, event | category | flops | bytes accessed | tf_op | source)
XLA Modules:
  0.0 719.5 jit_solution(1257271569724146589)
XLA Ops:
  0.7 0.1 pad.2.clone
  0.7 0.7 convert_element_type.27
  1.4 0.7 convert_element_type.28
  2.1 0.7 broadcast_in_dim.25
  2.8 0.7 broadcast_in_dim.26
  3.5 0.7 maximum_convert_fusion.refs_2_
  4.1 0.2 multiply_cosine_fusion
  4.3 0.6 pad_maximum_fusion.refs_1_
  5.0 694.2 %shard_map.212 = (bf16[256,2048]{1,0:T(8,128)(2,1)}, f32[256,2048]{1,0:T(8,128)}, f32[8,512]{1,0:T(8,128)}, bf16[2816,512]{1,0:T(8,128)(2,1)}, bf16[512,2816]{1,...) custom-call(bf16[1,256,2048]{2,1,0:T(8,128)(2,1)} %refs_0_.1, ...), custom_call_target="tpu_custom_call" | custom-call | tf_op jit(solution)/shard_map/pallas_call | solution.py:1075
  699.2 0.0 copy-start.4
  699.2 1.4 fusion.1
  700.6 1.8 fusion
  702.4 0.0 copy-start.2
  702.4 2.9 convert_element_type.30
  705.3 0.0 copy-done.4
  705.3 1.6 convert_element_type.32
  707.0 0.0 copy-done.2
  707.0 0.0 copy-start.1
  707.0 2.9 convert_element_type.33
  709.9 0.0 copy-done.1
  709.9 0.0 copy-start
  709.9 2.9 convert_element_type.34
  712.9 0.0 copy-done
  712.9 0.0 copy-start.5
  712.9 3.4 convert_element_type.35
  716.2 0.0 copy-done.5
  716.2 0.0 copy-start.3
  716.2 1.0 copy.26
  717.2 1.0 copy-done.3
  718.2 1.3 copy.27
  (3 shorter events, 0.0 us)
Async XLA Ops:
  699.2 6.2 copy-start.4
  702.4 4.6 copy-start.2
  707.0 2.9 copy-start.1
  709.9 2.9 copy-start
  712.9 3.4 copy-start.5
  716.2 2.0 copy-start.3

commit v2 on v1

--- a/solution.py
+++ b/solution.py
@@ -241,12 +241,24 @@
 T, W, H, TILE = 256, 2048, 1024, 128
 MAIN, WIN = 640, 768
 GRADS = (("d", 2816, 512), ("g", 512, 2816), ("u", 512, 2816), ("o", 1024, 512), ("q", 512, 1024), ("k", 512, 256))
-CHUNKS = [
-    (name, r, c, min(512, rows - r), min(512, cols - c))
-    for name, rows, cols in GRADS
-    for r in range(0, rows, 512)
-    for c in range(0, cols, 512)
-]
+PART = 384
+
+
+def chunk_list():
+    chunks = []
+    for name in "dgu":
+        for which in "AB":
+            for j in range(4):
+                begin = (11 * j + 1) // 2 * TILE
+                size = (11 * j + 12) // 2 * TILE - begin
+                at, size = (begin, PART) if which == "A" else (begin + PART, size - PART)
+                chunks.append((name + which, name) + ((at, 0, size, 512) if name == "d" else (0, at, 512, size)))
+    chunks += [("o", "o", r, 0, 512, 512) for r in (0, 512)]
+    chunks += [("q", "q", 0, c, 512, 512) for c in (0, 512)]
+    return chunks + [("k", "k", 0, 0, 512, 256)]
+
+
+CHUNKS = chunk_list()
 MESH = pl.DeviceIdType.MESH
 
 
@@ -277,7 +289,7 @@
     first, left, cross, total = ({name: next(names) for name, _, _ in GRADS} for _ in range(4))
     (x1, x2, ct, dh, w_qkv, w_o, w_g, w_u, w_d, act, dg, du, q_buf, kv_all, ob) = take(15)
     (ps, pr, rr, yo, hid, d_hid, xv, tb, ga, ids, r1s, r2s, ss_own, ss_other, lse, bias) = take(16)
-    (gs_d, kv_g, la, lb, ring, tt, d_kv, d_kv_recv, out_s, g_sum, g_plane, g_column, g_whole) = take(13)
+    (gs_d, kv_g, d_kv, d_kv_recv, out_s, g_sum, g_plane, g_column, g_whole) = take(9)
     send_sem, recv_sem, local_sem, credit = take(4)
     f, z, t = lax.axis_index("fsdp"), lax.axis_index("ctx"), lax.axis_index("tp")
     sems = iter(range(10**6))
@@ -322,72 +334,98 @@
     def starts(r):
         return (11 * r + 1) // 2
 
-    def weight_moves(k, s0, wait_side):
+    def weight_moves(k, taking):
         r = flip(f, k)
-        mine = f if not wait_side else r
-        rows = pl.ds(al(mine * 512, 512), 512)
-        begin = al(starts(r) * TILE, TILE) if not wait_side else al(starts(f) * TILE, TILE)
+        sender, taker = (r, f) if taking else (f, r)
+        rows = pl.ds(al(sender * 512, 512), 512)
+        row_part = pl.ds(al(sender * 512 + z * TILE, TILE), TILE)
+        own_part = pl.ds(al(z * TILE, TILE), TILE)
+        begin = al(starts(taker) * TILE, TILE)
         tail = al(begin + MAIN, TILE)
-        col = al((r if not wait_side else f) * T, T)
-        return {
-            "qkv": [(wq.at[:, pl.ds(col, T)], w_qkv.at[rows, pl.ds(0, T)]), (wk, w_qkv.at[rows, pl.ds(T, TILE)]), (wv, w_qkv.at[rows, pl.ds(T + TILE, TILE)])],
+        col = al(taker * T, T)
+        moves = {
             "o": [(wo.at[pl.ds(col, T), :], w_o.at[:, rows])],
-            "gu": [(wg.at[:, pl.ds(begin, MAIN)], w_g.at[rows, pl.ds(0, MAIN)]), (wu.at[:, pl.ds(begin, MAIN)], w_u.at[rows, pl.ds(0, MAIN)])],
-            "d": [(wd.at[pl.ds(begin, MAIN), :], w_d.at[pl.ds(0, MAIN), rows])],
-            "gu_tail": [(wg.at[:, pl.ds(tail, TILE)], w_g.at[rows, pl.ds(MAIN, TILE)]), (wu.at[:, pl.ds(tail, TILE)], w_u.at[rows, pl.ds(MAIN, TILE)])],
-            "d_tail": [(wd.at[pl.ds(tail, TILE), :], w_d.at[pl.ds(MAIN, TILE), rows])],
+            "g": [(wg.at[:, pl.ds(begin, MAIN)], w_g.at[rows, pl.ds(0, MAIN)])],
+            "g+": [(wg.at[:, pl.ds(tail, TILE)], w_g.at[rows, pl.ds(MAIN, TILE)])],
         }
-
-    w_sem = {(key, k, i): next(sems) for key, c in (("qkv", 3), ("o", 1), ("gu", 2), ("d", 1), ("gu_tail", 2), ("d_tail", 1)) for k in (1, 2, 3) for i in range(c)}
-    w_local = {(key, i): next(local_count) for key, c in (("qkv", 3), ("o", 1), ("gu", 2), ("d", 1), ("gu_tail", 2), ("d_tail", 1)) for i in range(c)}
+        from_rows, to_rows = (pl.ds(0, 512), rows) if k == 0 else (own_part, row_part)
+        moves["qkv"] = [
+            (wq.at[from_rows, pl.ds(col, T)], w_qkv.at[to_rows, pl.ds(0, T)]),
+            (wk.at[from_rows, :], w_qkv.at[to_rows, pl.ds(T, TILE)]),
+            (wv.at[from_rows, :], w_qkv.at[to_rows, pl.ds(T + TILE, TILE)]),
+        ]
+        if k == 0:
+            moves["u"] = [(wu.at[:, pl.ds(begin, MAIN)], w_u.at[rows, pl.ds(0, MAIN)])]
+            moves["u+"] = [(wu.at[:, pl.ds(tail, TILE)], w_u.at[rows, pl.ds(MAIN, TILE)])]
+            moves["d"] = [(wd.at[pl.ds(begin, MAIN), :], w_d.at[pl.ds(0, MAIN), rows])]
+            moves["d+"] = [(wd.at[pl.ds(tail, TILE), :], w_d.at[pl.ds(MAIN, TILE), rows])]
+        else:
+            moves["u"] = [(wu.at[own_part, pl.ds(begin, MAIN)], w_u.at[row_part, pl.ds(0, MAIN)])]
+            moves["u+"] = [(wu.at[own_part, pl.ds(tail, TILE)], w_u.at[row_part, pl.ds(MAIN, TILE)])]
+            moves["d"] = [(wd.at[pl.ds(begin, MAIN), own_part], w_d.at[pl.ds(0, MAIN), row_part])]
+            moves["d+"] = [(wd.at[pl.ds(tail, TILE), own_part], w_d.at[pl.ds(MAIN, TILE), row_part])]
+        return moves
+
+    w_counts = (("qkv", 3), ("o", 1), ("g", 1), ("g+", 1), ("u", 1), ("u+", 1), ("d", 1), ("d+", 1))
+    w_sem = {(key, k, i): next(sems) for key, c in w_counts for k in (1, 2, 3) for i in range(c)}
+    w_local = {(key, i): next(local_count) for key, c in w_counts for i in range(c)}
+
+    def weights_each(key, taking, run):
+        for k in (1, 2, 3):
+            moves = weight_moves(k, taking)
+            for i, (src, dst) in enumerate(moves[key]):
+                run(remote(src, dst, w_sem[key, k, i], plane(k)))
+            if key + "+" in moves:
+
+                @pl.when((f if taking else flip(f, k)) % 2 == 0)
+                def _():
+                    (src, dst), = moves[key + "+"]
+                    run(remote(src, dst, w_sem[key + "+", k, 0], plane(k)))
 
     def weights_start(key):
-        for k in (1, 2, 3):
-            for i, (src, dst) in enumerate(weight_moves(k, 0, False)[key]):
-                remote(src, dst, w_sem[key, k, i], plane(k)).start()
-            if key in ("gu", "d"):
-
-                @pl.when(flip(f, k) % 2 == 0)
-                def _():
-                    for i, (src, dst) in enumerate(weight_moves(k, 0, False)[key + "_tail"]):
-                        remote(src, dst, w_sem[key + "_tail", k, i], plane(k)).start()
+        weights_each(key, False, lambda cp: cp.start())
+
+    def weights_wait(key):
+        weights_each(key, True, lambda cp: cp.wait_recv())
+
+    def weights_drain():
+        for key in ("qkv", "o", "g", "u", "d"):
+            weights_each(key, False, lambda cp: cp.wait_send())
 
     def weights_own(wait):
-        moves = weight_moves(0, 0, False)
-        for key in ("qkv", "o", "gu", "d"):
+        moves = weight_moves(0, False)
+
+        def run(key):
             for i, (src, dst) in enumerate(moves[key]):
                 cp = here(src, dst, w_local[key, i])
                 cp.wait() if wait else cp.start()
 
+        for key in ("qkv", "o", "g", "u", "d"):
+            run(key)
+
         @pl.when(f % 2 == 0)
         def _():
-            for key in ("gu_tail", "d_tail"):
-                for i, (src, dst) in enumerate(moves[key]):
-                    cp = here(src, dst, w_local[key, i])
-                    cp.wait() if wait else cp.start()
-
-    def weights_wait(key):
+            for key in ("g+", "u+", "d+"):
+                run(key)
+
+    y_sem = {(key, k, j): next(sems) for key in ("qkv", "u", "d") for k in (1, 2, 3) for j in (1, 2, 3)}
+
+    def column_each(key, taking, run):
         for k in (1, 2, 3):
-            for i, (src, dst) in enumerate(weight_moves(k, 0, True)[key]):
-                remote(src, dst, w_sem[key, k, i], plane(k)).wait_recv()
-            if key in ("gu", "d"):
-
-                @pl.when(f % 2 == 0)
-                def _():
-                    for i, (src, dst) in enumerate(weight_moves(k, 0, True)[key + "_tail"]):
-                        remote(src, dst, w_sem[key + "_tail", k, i], plane(k)).wait_recv()
-
-    def weights_drain():
-        for key in ("qkv", "o", "gu", "d"):
-            for k in (1, 2, 3):
-                for i, (src, dst) in enumerate(weight_moves(k, 0, False)[key]):
-                    remote(src, dst, w_sem[key, k, i], plane(k)).wait_send()
-                if key in ("gu", "d"):
-
-                    @pl.when(flip(f, k) % 2 == 0)
-                    def _():
-                        for i, (src, dst) in enumerate(weight_moves(k, 0, False)[key + "_tail"]):
-                            remote(src, dst, w_sem[key + "_tail", k, i], plane(k)).wait_send()
+            for j in (1, 2, 3):
+                from_z = flip(z, j) if taking else z
+                part = pl.ds(al(flip(f, k) * 512 + from_z * TILE, TILE), TILE)
+
+                def move(size):
+                    ref = w_u.at[part, pl.ds(0, size)] if key == "u" else w_d.at[pl.ds(0, size), part]
+                    run(remote(ref, ref, y_sem[key, k, j], column(j)))
+
+                if key == "qkv":
+                    ref = w_qkv.at[part, :]
+                    run(remote(ref, ref, y_sem[key, k, j], column(j)))
+                    continue
+                pl.when(f % 2 == 0)(functools.partial(move, WIN))
+                pl.when(f % 2 == 1)(functools.partial(move, MAIN))
 
     g_sem = [[next(sems) for _ in range(3)] for _ in range(4)]
     f_sem = [[next(sems) for _ in range(4)] for _ in range(4)]
@@ -465,13 +503,15 @@
         x1[pl.ds(al(f * T + i * STEP, STEP), STEP), :] = (xs * scale * ga[0:1, :]).astype(BF)
 
     gather_start(0, x1, False)
-    weights_start("o")
+    weights_wait("qkv")
+    column_each("qkv", False, lambda cp: cp.start())
+    for key in "oudg":
+        weights_start(key)
     for k in (1, 2, 3):
         dst = tb.at[flip(f, k)]
         remote(dst, dst, t_sem[k - 1], plane(k)).wait_recv()
     weights_own(True)
-    weights_wait("qkv")
-    weights_start("gu")
+    column_each("qkv", True, lambda cp: cp.wait_recv())
 
     lane = lax.broadcasted_iota(jnp.int32, (T, TILE), 1)
     low_lane = lane < HD
@@ -516,12 +556,13 @@
     for k in (1, 2, 3):
         remote(kv_all.at[z], kv_all.at[z], z_sem[k - 1][0], column(k)).start()
         remote(ids.at[z], ids.at[z], z_sem[k - 1][1], column(k)).start()
-    gather_start(1, ct, False, cot_in.at[0, :, half])
     for k in (1, 2, 3):
         zz = flip(z, k)
         remote(kv_all.at[zz], kv_all.at[zz], z_sem[k - 1][0], column(k)).wait_recv()
         remote(ids.at[zz], ids.at[zz], z_sem[k - 1][1], column(k)).wait_recv()
     lc.wait()
+    weights_wait("u")
+    column_each("u", False, lambda cp: cp.start())
 
     low_keys = lax.broadcasted_iota(jnp.int32, (4 * T, TILE), 1) < HD
 
@@ -560,8 +601,8 @@
                 mixed.append(nn(values_t, weights))
             ob[rows_of(s), i * TILE : (i + 1) * TILE] = jnp.transpose(jnp.concatenate(mixed, 0)).astype(BF)
 
-    p_sem = [[next(sems) for _ in range(4)] for _ in range(4)]
-    s_sem = [[next(sems) for _ in range(3)] for _ in range(4)]
+    p_sem = [[next(sems) for _ in range(4)]] * 4
+    s_sem = [[next(sems) for _ in range(3)]] * 4
     COLS = 256
 
     def scatter_start(u, product):
@@ -612,9 +653,9 @@
         remote(ss_own.at[u], ss_other.at[u], n_sem[u], core).start()
         remote(ss_own.at[u], ss_other.at[u], n_sem[u], core).wait()
 
+    weights_wait("d")
+    column_each("d", False, lambda cp: cp.start())
     weights_wait("o")
-    weights_wait("gu")
-    weights_start("d")
     scatter_start(0, lambda b, c: nn(ob[rows_of(b), :], w_o[:, pl.ds(al(c, COLS), COLS)]))
     scatter_wait(0)
 
@@ -634,10 +675,9 @@
         x2[pl.ds(al(f * T + i * STEP, STEP), STEP), half] = (hid[sub(i), :] * scale * gain_two).astype(BF)
 
     gather_start(2, x2, True)
-    gather_forward(1, ct)
-    for k in (1, 2, 3):
-        gather_take(1, ct, k)
-    weights_wait("d")
+    gather_start(1, ct, False, cot_in.at[0, :, half])
+    weights_wait("g")
+    column_each("u", True, lambda cp: cp.wait_recv())
     gather_forward(2, x2)
     gather_take(2, x2, 0)
 
@@ -651,12 +691,11 @@
             cols = pl.ds(al(j * UNITS, UNITS), UNITS)
             gate = nn(x2[rows_of(b), :], w_g[:, cols])
             up = nn(x2[rows_of(b), :], w_u[:, cols])
-            back = nt(ct[rows_of(b), :], w_d[cols, :])
             sigma = jax.nn.sigmoid(gate)
             silu = gate * sigma
             act[rows_of(b), cols] = (silu * up).astype(BF)
-            dg[rows_of(b), cols] = (back * up * sigma * (1.0 + gate * (1.0 - sigma))).astype(BF)
-            du[rows_of(b), cols] = (back * silu).astype(BF)
+            dg[rows_of(b), cols] = (up * sigma * (1.0 + gate * (1.0 - sigma))).astype(BF)
+            du[rows_of(b), cols] = silu.astype(BF)
 
     feed_block(0)
     for k in (1, 2, 3):
@@ -666,41 +705,46 @@
     def _(k):
         feed_block(k)
 
-    e_sem = {(name, k, i): next(sems) for name in "dguoqk" for k in (1, 2, 3) for i in range(2)}
-    e_local = {(name, i): next(local_count) for name in "dguoqk" for i in range(2)}
-    mine = al(starts(f) * TILE, TILE)
+    gather_forward(1, ct)
+    for k in (1, 2, 3):
+        gather_take(1, ct, k)
+
+    GROUPS = ("dA", "dB", "gA", "gB", "uA", "uB", "o", "q", "k")
+    e_sem = {(name, i): [next(sems) for _ in range(3)][0] for name in GROUPS for i in range(2 if name[-1] == "B" else 1)}
+    e_local = {(name, i): next(local_count) for name in GROUPS for i in range(2 if name[-1] == "B" else 1)}
 
     def stage(name, k):
         if name == "d":
-            return gs_d.at[pl.ds(k * WIN, WIN), :]
+            return gs_d.at[pl.ds(al(k * WIN, WIN), WIN), :]
         if name in "gu":
-            return ct.at[pl.ds((k // 2) * 512, 512), pl.ds((k % 2) * H, WIN)]
+            return ct.at[pl.ds(al((k // 2) * 512, 512), 512), pl.ds(al((k % 2) * H, H), WIN)]
         if name == "o":
-            return gs_d.at[pl.ds(k * WIN, T), :]
-        return x2.at[pl.ds((k // 2) * 512, 512), pl.ds((k % 2) * 512 + (0 if name == "q" else T), T)]
-
-    def grad_moves(name, k, sender):
+            return gs_d.at[pl.ds(al(k * WIN, WIN), T), :]
+        return x2.at[pl.ds(al((k // 2) * 512, 512), 512), pl.ds(al((k % 2) * 512 + (0 if name == "q" else T), T), T)]
+
+    def grad_moves(group, k, sender):
+        name = group[0]
         buf, begin = stage(name, k), al(starts(sender) * TILE, TILE)
-        tail = al(begin + MAIN, TILE)
-        if name == "d":
-            return [(buf.at[pl.ds(0, MAIN), :], first["d"].at[pl.ds(begin, MAIN), :]), (buf.at[pl.ds(MAIN, TILE), :], first["d"].at[pl.ds(tail, TILE), :])]
-        if name in "gu":
-            return [(buf.at[:, pl.ds(0, MAIN)], first[name].at[:, pl.ds(begin, MAIN)]), (buf.at[:, pl.ds(MAIN, TILE)], first[name].at[:, pl.ds(tail, TILE)])]
+        if name in "dgu":
+            parts = [(0, PART)] if group[1] == "A" else [(PART, MAIN - PART), (MAIN, TILE)]
+            if name == "d":
+                return [(buf.at[pl.ds(c, size), :], first["d"].at[pl.ds(al(begin + c, TILE), size), :]) for c, size in parts]
+            return [(buf.at[:, pl.ds(c, size)], first[name].at[:, pl.ds(al(begin + c, TILE), size)]) for c, size in parts]
         if name == "o":
             return [(buf, first["o"].at[rows_of(sender), :])]
         if name == "q":
             return [(buf, first["q"].at[:, rows_of(sender)])]
         return [(buf, kv_g.at[k - 1])]
 
-    def grad_send(name, k, act_on, only_wait=False):
-        for i, (src, dst) in enumerate(grad_moves(name, k, f)):
+    def grad_send(group, k, act_on):
+        for i, (src, dst) in enumerate(grad_moves(group, k, f)):
 
             def run(i=i, src=src, dst=dst):
-                if k == 0:
-                    cp = here(src, dst, e_local[name, i])
+                if isinstance(k, int) and k == 0:
+                    cp = here(src, dst, e_local[group, i])
                     cp.wait() if act_on == "wait" else cp.start()
                 else:
-                    cp = remote(src, dst, e_sem[name, k, i], plane(k))
+                    cp = remote(src, dst, e_sem[group, i] + k - 1, plane(k))
                     cp.wait_send() if act_on == "wait" else cp.start()
 
             if i == 0:
@@ -708,65 +752,100 @@
             else:
                 pl.when(f % 2 == 0)(run)
 
-    def grad_take(name):
+    def grad_take(group):
         for k in (1, 2, 3):
             sender = flip(f, k)
-            for i, (src, dst) in enumerate(grad_moves(name, k, sender)):
+            for i, (src, dst) in enumerate(grad_moves(group, k, sender)):
 
                 def run(i=i, src=src, dst=dst):
-                    remote(src, dst, e_sem[name, k, i], plane(k)).wait_recv()
+                    remote(src, dst, e_sem[group, i] + k - 1, plane(k)).wait_recv()
 
                 if i == 0:
                     run()
                 else:
                     pl.when(sender % 2 == 0)(run)
 
+    def sent(*groups):
+        for group in groups:
+            for k in (1, 2, 3):
+                grad_send(group, k, "wait")
+
     def block_cols(k):
         return pl.ds(al(flip(f, k) * 512, 512), 512)
 
-    for k in (1, 2, 3, 0):
-
+    def each_owner(run):
+        @pl.loop(1, 4)
+        def _(k):
+            run(k)
+
+        run(0)
+
+    def down_grads(which):
+        c = 0 if which == "A" else PART
+
+        def run(k):
+            stage("d", k)[c : c + PART, :] = tn(act[:, c : c + PART], ct[:, block_cols(k)]).astype(BF)
+            grad_send("d" + which, k, "start")
+
+        each_owner(run)
+
+    def feed_grads(name, which, right):
+        c = 0 if which == "A" else PART
+
+        def run(k):
+            @pl.loop(0, 2)
+            def _(i):
+                xs = x2[:, pl.ds(al(flip(f, k) * 512 + i * T, T), T)]
+                stage(name, k)[pl.ds(al(i * T, T), T), c : c + PART] = tn(xs, right[:, c : c + PART]).astype(BF)
+
+            grad_send(name + which, k, "start")
+
+        each_owner(run)
+
+    down_grads("A")
+
+    column_each("d", True, lambda cp: cp.wait_recv())
+
+    @pl.loop(0, 4)
+    def _(b):
         @pl.loop(0, WIN // UNITS)
         def _(j):
             cols = pl.ds(al(j * UNITS, UNITS), UNITS)
-            gs_d[pl.ds(al(k * WIN + j * UNITS, UNITS), UNITS), :] = tn(act[:, cols], ct[:, block_cols(k)]).astype(BF)
-
-        grad_send("d", k, "start")
+            back = nt(ct[rows_of(b), :], w_d[cols, :])
+            dg[rows_of(b), cols] = (back * dg[rows_of(b), cols].astype(F32)).astype(BF)
+            du[rows_of(b), cols] = (back * du[rows_of(b), cols].astype(F32)).astype(BF)
 
     scatter_start(1, lambda b, c: nt(dg[rows_of(b), :], w_g[pl.ds(al(c, COLS), COLS), :]) + nt(du[rows_of(b), :], w_u[pl.ds(al(c, COLS), COLS), :]))
-
-    gather_drain(1, ct, False, cot_in.at[0, :, half])
-    def feed_grads(name, right):
-        for k in (1, 2, 3, 0):
-
-            @pl.loop(0, 2)
-            def _(i):
-                xs = x2[:, pl.ds(al(flip(f, k) * 512 + i * T, T), T)]
-                stage(name, k)[pl.ds(al(i * T, T), T), :] = tn(xs, right[...]).astype(BF)
-
-            grad_send(name, k, "start")
-
-    feed_grads("g", dg)
-
     end = (z == 0) | (z == 3)
     middle = (z == 1) | (z == 2)
     next_in = (f, jnp.where(z < 2, 1, 2), t)
     next_out = (f, jnp.where(z < 2, 0, 3), t)
     facing = (f, 3 - z, t)
-    l_sem = [[next(sems) for _ in range(3)] for _ in CHUNKS]
+    across = [next(sems) for _ in range(6)]
+    l_sem = [[next(sems), across[i % 6], next(sems)] for i in range(len(CHUNKS))]
     v_sem = [next(local_count) for _ in range(2)]
-    o_sem = [next(local_count) for _ in CHUNKS]
-    DEPTH = 2
+    o_sem = [next(local_count) for _ in range(4)]
+    DEPTH, LAG = 3, 2
+
+    def square(buf, i):
+        return buf.at[pl.ds(i * 512, 512), pl.ds(0, 512)]
+
+    ring, la = [square(w_u, i) for i in range(DEPTH)], square(w_u, 3)
+    tt, lb = [square(w_g, i) for i in range(2)], square(w_g, 2)
+
+    def d_kv_place(j):
+        return w_g.at[pl.ds(al(j // 2 * 4 * T, T), 4 * T), pl.ds(al(512 + j % 2 * TILE, TILE), TILE)]
+
 
     def window(arrays, i):
-        name, r, c, rows, cols = CHUNKS[i]
+        _, name, r, c, rows, cols = CHUNKS[i]
         return arrays[name].at[pl.ds(r, rows), pl.ds(c, cols)]
 
-    def line_send(name):
+    def line_send(group):
         @pl.when(end)
         def _():
             for i, chunk in enumerate(CHUNKS):
-                if chunk[0] == name:
+                if chunk[0] == group:
                     remote(window(first, i), window(left, i), l_sem[i][0], next_in).start()
 
     def add_into(dst, a, b, rows, cols):
@@ -776,9 +855,9 @@
             dst[at, pl.ds(0, cols)] = (a[at, pl.ds(0, cols)].astype(F32) + b[at, pl.ds(0, cols)].astype(F32)).astype(BF)
 
     def line_one(i):
-        name, r, c, rows, cols = CHUNKS[i]
+        _, name, r, c, rows, cols = CHUNKS[i]
         part = (pl.ds(0, rows), pl.ds(0, cols))
-        a, b, keep = la.at[part], lb.at[part], ring.at[i % DEPTH]
+        a, b, keep = la.at[part], lb.at[part], ring[i % DEPTH]
 
         @pl.when(middle)
         def _():
@@ -793,9 +872,9 @@
             remote(keep.at[part], window(cross, i), l_sem[i][1], facing).start()
 
     def line_two(i):
-        name, r, c, rows, cols = CHUNKS[i]
+        _, name, r, c, rows, cols = CHUNKS[i]
         part = (pl.ds(0, rows), pl.ds(0, cols))
-        keep, done = ring.at[i % DEPTH], tt.at[i % 2]
+        keep, done = ring[i % DEPTH], tt[i % 2]
 
         @pl.when(middle)
         def _():
@@ -807,32 +886,38 @@
             get.wait()
             add_into(done, keep, lb, rows, cols)
             remote(done.at[part], window(total, i), l_sem[i][2], next_out).start()
-            here(done.at[part], window(total, i), o_sem[i]).start()
+            here(done.at[part], window(total, i), o_sem[i % 4]).start()
 
     def line_out(i):
-        name, r, c, rows, cols = CHUNKS[i]
-        done = tt.at[i % 2].at[pl.ds(0, rows), pl.ds(0, cols)]
+        _, name, r, c, rows, cols = CHUNKS[i]
+        done = tt[i % 2].at[pl.ds(0, rows), pl.ds(0, cols)]
         remote(done, window(total, i), l_sem[i][2], next_out).wait_send()
-        here(done, window(total, i), o_sem[i]).wait()
-
-    pumped = [0]
-
-    def pump(name):
-        while pumped[0] < len(CHUNKS) and CHUNKS[pumped[0]][0] == name:
-            i = pumped[0]
-            line_one(i)
-            if i >= 1:
-                line_two(i - 1)
-            pumped[0] += 1
-
-    def grad_ready(name):
-        grad_take(name)
-        grad_send(name, 0, "wait")
-        line_send(name)
-
-    grad_ready("d")
+        here(done, window(total, i), o_sem[i % 4]).wait()
+
+    pumped, ready = [0], set()
+
+    def pump(count):
+        for i in range(pumped[0], pumped[0] + count):
+            if i < len(CHUNKS):
+                assert CHUNKS[i][0] in ready
+                line_one(i)
+            if LAG <= i < len(CHUNKS) + LAG:
+                line_two(i - LAG)
+        pumped[0] += count
+
+    def grad_ready(group):
+        grad_take(group)
+        grad_send(group, 0, "wait")
+        line_send(group)
+        ready.add(group)
+
+    grad_ready("dA")
+    down_grads("B")
+    gather_drain(1, ct, False, cot_in.at[0, :, half])
+    feed_grads("g", "A", dg)
+    column_each("u", False, lambda cp: cp.wait_send())
+    pump(2)
     scatter_wait(1)
-
     lh.wait()
 
     def norm_two_back(i, carry):
@@ -856,28 +941,29 @@
         dh[pl.ds(al(f * T + i * STEP, STEP), STEP), half] = rows.astype(BF)
 
     gather_start(3, dh, True)
-    grad_ready("g")
+    feed_grads("g", "B", dg)
+    pump(1)
+    grad_ready("dB")
+    pump(2)
+    grad_ready("gA")
+    pump(4)
     gather_forward(3, dh)
-    pump("d")
     for k in range(4):
         gather_take(3, dh, k)
-    for k in (1, 2, 3):
-        grad_send("g", k, "wait")
-    feed_grads("u", du)
-
-    for k in (1, 2, 3):
-        grad_send("d", k, "wait")
-    for k in (1, 2, 3, 0):
-        gs_d[k * WIN : k * WIN + T, :] = tn(ob[...], dh[:, block_cols(k)]).astype(BF)
+    pump(1)
+    sent("dA", "dB")
+
+    def out_grads(k):
+        stage("o", k)[...] = tn(ob[...], dh[:, block_cols(k)]).astype(BF)
         grad_send("o", k, "start")
+
+    each_owner(out_grads)
 
     @pl.loop(0, 4)
     def _(b):
         ob[rows_of(b), :] = nt(dh[rows_of(b), :], w_o[...]).astype(BF)
 
     d_ob, d_qkv = ob, dg
-    scatter_start(2, lambda b, c: nn(act[rows_of(b), :], w_d[:, pl.ds(al(c, COLS), COLS)]))
-
     gather_drain(2, x2, True)
 
     def attend_back(s):
@@ -909,41 +995,30 @@
             own = jnp.where(z == j, both[j * T : (j + 1) * T, :], own)
         d_kv[s, :, :] = own
         for j in range(4):
-            x2[rows_of(s), H + j * TILE : H + (j + 1) * TILE] = both[j * T : (j + 1) * T, :].astype(BF)
-
-    @pl.loop(0, 2)
-    def _(s):
-        attend_back(s)
-
-    grad_ready("u")
-    pump("g")
-    scatter_wait(2)
-
-    @pl.loop(0, T // STEP)
-    def _(i):
-        out_s[sub(i), :] = (hid[sub(i), :] + scattered(i)).astype(BF)
-
-    for k in (1, 2, 3):
-        pl.semaphore_signal(credit, inc=1, device_id=plane(k), device_id_type=MESH)
-    pl.semaphore_signal(credit, inc=1, device_id=core, device_id_type=MESH)
-    out_local = here(out_s, out_ref.at[:, half], next(local_count))
-    out_local.start()
-    out_remote = remote(out_s, out_ref.at[:, half], next(sems), core)
-    out_remote.start()
-
-    @pl.loop(2, 4)
-    def _(s):
-        attend_back(s)
-
+            d_kv_place(j)[rows_of(s), :] = both[j * T : (j + 1) * T, :].astype(BF)
+
+    attend_back(0)
+    pump(1)
+    attend_back(1)
+    grad_ready("gB")
+    pump(1)
+    sent("gA", "gB")
+    feed_grads("u", "A", du)
+    attend_back(2)
+    pump(1)
+    attend_back(3)
     k_sem = [next(sems) for _ in range(3)]
     for k in (1, 2, 3):
-        remote(x2.at[:, pl.ds(al(H + flip(z, k) * TILE, TILE), TILE)], d_kv_recv.at[k - 1], k_sem[k - 1], column(k)).start()
+        remote(d_kv_place(flip(z, k)), d_kv_recv.at[k - 1], k_sem[k - 1], column(k)).start()
+    pump(1)
+    feed_grads("u", "B", du)
+    pump(1)
     grad_ready("o")
-    pump("u")
-    for k in (1, 2, 3):
-        remote(x2.at[:, pl.ds(al(H + flip(z, k) * TILE, TILE), TILE)], d_kv_recv.at[k - 1], k_sem[k - 1], column(k)).wait()
-
-    here_half = low_lane if False else (lane // HD) == kv_head
+    grad_ready("uA")
+    pump(3)
+    for k in (1, 2, 3):
+        remote(d_kv_place(flip(z, k)), d_kv_recv.at[k - 1], k_sem[k - 1], column(k)).wait()
+    here_half = (lane // HD) == kv_head
 
     @pl.loop(0, 4)
     def _(s):
@@ -957,19 +1032,23 @@
         d_qkv[rows_of(s), 2 * TILE : 3 * TILE] = jnp.where(here_half, d_key, 0.0).astype(BF)
         d_qkv[rows_of(s), 3 * TILE : 4 * TILE] = jnp.where(here_half, d_value, 0.0).astype(BF)
 
-    for k in (1, 2, 3, 0):
-
+    def qkv_grads(k):
         @pl.loop(0, 2)
         def _(i):
             xs = x1[:, pl.ds(al(flip(f, k) * 512 + i * T, T), T)]
-            x2[pl.ds(al((k // 2) * 512 + i * T, T), T), (k % 2) * 512 : (k % 2) * 512 + 512] = tn(xs, d_qkv[:, 0:512]).astype(BF)
+            grads = tn(xs, d_qkv[:, 0:512]).astype(BF)
+            stage("q", k)[pl.ds(al(i * T, T), T), :] = grads[:, 0:T]
+            stage("k", k)[pl.ds(al(i * T, T), T), :] = grads[:, T:]
 
         grad_send("q", k, "start")
-        if k:
+        if not (isinstance(k, int) and k == 0):
             grad_send("k", k, "start")
-    pl.semaphore_wait(credit, 4)
-    scatter_start(3, lambda b, c: nt(d_qkv[rows_of(b), 0:512], w_qkv[pl.ds(al(c, COLS), COLS), :]))
-    pump("o")
+
+    each_owner(qkv_grads)
+    pump(1)
+    scatter_start(2, lambda b, c: nt(d_qkv[rows_of(b), 0:512], w_qkv[pl.ds(al(c, COLS), COLS), :]))
+    grad_ready("uB")
+    pump(2)
     grad_ready("q")
     grad_take("k")
 
@@ -978,14 +1057,15 @@
         rows = x2[sub(i), T : 2 * T].astype(F32)
         for k in (1, 2, 3):
             rows = rows + kv_g[k - 1, sub(i), :].astype(F32)
-        la[sub(i), 0:T] = rows.astype(BF)
-
-    kv_copy = here(la.at[:, pl.ds(0, T)], first["k"], next(local_count))
+        x2[sub(i), T : 2 * T] = rows.astype(BF)
+
+    kv_copy = here(x2.at[pl.ds(0, 512), pl.ds(T, T)], first["k"], next(local_count))
     kv_copy.start()
     kv_copy.wait()
     line_send("k")
-    pump("q")
-    scatter_wait(3)
+    ready.add("k")
+    pump(4)
+    scatter_wait(2)
 
     def norm_one_back(i, carry):
         rows = scattered(i)
@@ -995,6 +1075,9 @@
         return carry + jnp.sum(rows * hat, axis=0, keepdims=True)
 
     g_sum[0:1, :] = lax.fori_loop(0, T // STEP, norm_one_back, jnp.zeros((1, H), F32))
+    for k in (1, 2, 3):
+        pl.semaphore_signal(credit, inc=1, device_id=plane(k), device_id_type=MESH)
+    pl.semaphore_signal(credit, inc=1, device_id=core, device_id_type=MESH)
     core_sums(2)
 
     q_sem = [[next(sems) for _ in range(3)] for _ in range(2)]
@@ -1007,19 +1090,32 @@
         scale = r1s[sub(i), 0:1]
         hat = xv[sub(i), half].astype(F32) * scale
         mean = (ss_own[2, sub(i), 0:1] + ss_other[2, sub(i), 0:1]) * (1.0 / W)
-        yo[sub(i), :] = d_hid[sub(i), :] + scale * (yo[sub(i), :] * gain_one - hat * mean)
-
-    in_local = here(yo, in_grad_ref.at[:, half], next(local_count))
+        d_hid[sub(i), :] = d_hid[sub(i), :] + scale * (yo[sub(i), :] * gain_one - hat * mean)
+
+    in_local = here(d_hid, in_grad_ref.at[:, half], next(local_count))
     in_local.start()
-    in_remote = remote(yo, in_grad_ref.at[:, half], next(sems), core)
+    in_remote = remote(d_hid, in_grad_ref.at[:, half], next(sems), core)
     in_remote.start()
+    pump(1)
+    pl.semaphore_wait(credit, 4)
+    scatter_start(3, lambda b, c: nn(act[rows_of(b), :], w_d[:, pl.ds(al(c, COLS), COLS)]))
+    pump(2)
     for k in (1, 2, 3):
         remote(g_sum, g_plane.at[flip(f, k)], q_sem[0][k - 1], plane(k)).wait_recv()
     g_column[z, :, :] = ((g_plane[0, :, :] + g_plane[1, :, :]) + g_plane[2, :, :]) + g_plane[3, :, :]
     for k in (1, 2, 3):
         remote(g_column.at[z], g_column.at[z], q_sem[1][k - 1], column(k)).start()
-    pump("k")
-    line_two(len(CHUNKS) - 1)
+    scatter_wait(3)
+
+    @pl.loop(0, T // STEP)
+    def _(i):
+        out_s[sub(i), :] = (hid[sub(i), :] + scattered(i)).astype(BF)
+
+    out_local = here(out_s, out_ref.at[:, half], next(local_count))
+    out_local.start()
+    out_remote = remote(out_s, out_ref.at[:, half], next(sems), core)
+    out_remote.start()
+    pump(2)
     for k in (1, 2, 3):
         remote(g_column.at[z], g_column.at[flip(z, k)], q_sem[1][k - 1], column(k)).wait_recv()
     g_whole[:, half] = ((g_column[0, :, :] + g_column[1, :, :]) + g_column[2, :, :]) + g_column[3, :, :]
@@ -1028,6 +1124,7 @@
     w_move.wait()
     gain_move = here(g_whole.at[:, pl.ds(al(f * 512, 512), 512)], gain_ref, next(local_count))
     gain_move.start()
+    pump(len(CHUNKS) + LAG - pumped[0])
 
     @pl.when(middle)
     def _():
@@ -1046,6 +1143,8 @@
     in_local.wait()
     in_remote.wait()
     weights_drain()
+    column_each("d", False, lambda cp: cp.wait_send())
+    column_each("qkv", False, lambda cp: cp.wait_send())
     gather_drain(0, x1, False)
     gather_drain(3, dh, True)
     for k in (1, 2, 3):
@@ -1055,12 +1154,12 @@
         remote(ids.at[z], ids.at[z], z_sem[k - 1][1], column(k)).wait_send()
         remote(g_sum, g_plane.at[f], q_sem[0][k - 1], plane(k)).wait_send()
         remote(g_column.at[z], g_column.at[z], q_sem[1][k - 1], column(k)).wait_send()
-        for name in "uoqk":
+        for name in ("uA", "uB", "o", "q", "k"):
             grad_send(name, k, "wait")
-    assert next(sems) <= REMOTE_SEMS and next(local_count) <= LOCAL_SEMS
-
-
-REMOTE_SEMS, LOCAL_SEMS = 400, 96
+    assert (next(sems), next(local_count)) == (REMOTE_SEMS, LOCAL_SEMS)
+
+
+REMOTE_SEMS, LOCAL_SEMS = 219, 37
 
 
 def layer_call(inputs, positions, blocks, cotangent, attn_gain, w_query, w_key, w_value, w_out, mlp_gain, w_gate, w_up, w_down):
@@ -1085,8 +1184,8 @@
             v((4, T, H), BF), v((4, T, H), BF), v((3, T, H), BF), v((T, H), F32), v((T, H), F32), v((T, H), F32), v((T, W), BF),
             v((4, 72, T), F32), v((8, W), F32), v((4, 8, T), F32), v((T, TILE), F32), v((T, TILE), F32),
             v((3, T, TILE), F32), v((3, T, TILE), F32), v((4, 8, T), F32), v((4 * T, T), BF),
-            v((4 * WIN, 512), BF), v((3, 512, T), BF), v((512, 512), BF), v((512, 512), BF),
-            v((2, 512, 512), BF), v((2, 512, 512), BF), v((4, T, TILE), F32), v((3, 4 * T, TILE), BF),
+            v((4 * WIN, 512), BF), v((3, 512, T), BF),
+            v((4, T, TILE), F32), v((3, 4 * T, TILE), BF),
             v((T, H), BF), v((8, H), F32), v((4, 8, H), F32), v((4, 8, H), F32), v((8, W), F32),
             pltpu.SemaphoreType.DMA((REMOTE_SEMS,)), pltpu.SemaphoreType.DMA((REMOTE_SEMS,)),
             pltpu.SemaphoreType.DMA((LOCAL_SEMS,)), pltpu.SemaphoreType.REGULAR,

time: 722 us -> 545 us (0.75)
  Pallas kernels: 694 us -> 517 us
    pallas_call x1, Pallas kernels: 694 us -> 517 us  [layer_call(): pl.pallas_call(layer_kernel, out_shape=[shape((T, W), BF), shape((T, W),...]
where the time goes in v2:
time: 545 us; the launch traced here: 542 us
  Pallas kernels  517 us (95%)
  other arithmetic  16.7 us (3%)
  local copies, waits for them, and re-layouts  7.95 us (1%)
    pallas_call x1, Pallas kernels, layer_call(): pl.pallas_call(layer_kernel, out_shape=[shape((T, W), BF), shape((T, W),...  517 us
    convert_element_type x5, other arithmetic, layer_call(): down, gate, up, out, query, kv = (r.astype(F32) for r in results[-6:])  13.8 us

profile of v2, /device:TPU:0, one launch (start us, length us, event | category | flops | bytes accessed | tf_op | source)
XLA Modules:
  0.0 542.1 jit_solution(17336332616381485626)
XLA Ops:
  0.7 0.1 pad.2.clone
  0.7 0.7 convert_element_type.27
  1.4 0.7 convert_element_type.28
  2.1 0.7 broadcast_in_dim.25
  2.8 0.7 broadcast_in_dim.26
  3.5 0.7 maximum_convert_fusion.refs_2_
  4.1 0.2 multiply_cosine_fusion
  4.3 0.6 pad_maximum_fusion.refs_1_
  5.0 516.8 %shard_map.212 = (bf16[256,2048]{1,0:T(8,128)(2,1)}, f32[256,2048]{1,0:T(8,128)}, f32[8,512]{1,0:T(8,128)}, bf16[2816,512]{1,0:T(8,128)(2,1)}, bf16[512,2816]{1,...) custom-call(bf16[1,256,2048]{2,1,0:T(8,128)(2,1)} %refs_0_.1, ...), custom_call_target="tpu_custom_call" | custom-call | tf_op jit(solution)/shard_map/pallas_call | solution.py:1174
  521.8 0.0 copy-start.4
  521.8 1.4 fusion.1
  523.2 1.8 fusion
  525.0 0.0 copy-start.2
  525.0 2.9 convert_element_type.30
  527.9 0.0 copy-done.4
  527.9 1.6 convert_element_type.32
  529.5 0.0 copy-done.2
  529.5 0.0 copy-start.1
  529.5 2.9 convert_element_type.33
  532.5 0.0 copy-done.1
  532.5 0.0 copy-start
  532.5 2.9 convert_element_type.34
  535.4 0.0 copy-done
  535.4 0.0 copy-start.5
  535.4 3.4 convert_element_type.35
  538.8 0.0 copy-done.5
  538.8 0.0 copy-start.3
  538.8 1.0 copy.26
  539.8 1.0 copy-done.3
  540.8 1.3 copy.27
  (3 shorter events, 0.0 us)
Async XLA Ops:
  521.8 6.2 %copy-start.4 = (bf16[1024,512]{1,0:T(8,128)(2,1)S(1)}, bf16[1024,512]{1,0:T(8,128)(2,1)}, u32[]{:S(2)}) copy-start(bf16[1024,512]{1,0:T(8,128)(2,1)} %get-tuple-element.25) | copy-start | bytes 3145732
  525.0 4.6 copy-start.2
  529.5 2.9 copy-start.1
  532.5 2.9 copy-start
  535.4 3.4 copy-start.5
  538.8 2.0 copy-start.3
